TPU v7x, 32 devices: a whole 2x2x4 slice. The times are simulated.
32 devices in a mesh: rep: 4 (over y, core), fsdp: 8 (over z, x).
Axes of the slice: x: 2, y: 2, z: 4, core: 2. Of those that a mesh axis runs over, the one named last changes fastest.
Arguments:
- query_rows: bfloat16 [4, 3072, 2560], P('rep', 'fsdp'), may hold values from -5 to 5
- key_rows: bfloat16 [4, 3072, 2560], P('rep', 'fsdp'), may hold values from -5 to 5
- value_rows: bfloat16 [4, 3072, 2560], P('rep', 'fsdp'), may hold values from -5 to 5
- residual_in: bfloat16 [4, 3072, 2560], P('rep', 'fsdp'), may hold values from -6 to 6
- out_grad: bfloat16 [4, 3072, 2560], P('rep', 'fsdp'), may hold values from -6 to 6
- doc_ids: int32 [4, 3072], P('rep', 'fsdp'), may hold values from 0 to 47, never falling along the last dimension, each value on 1 to 256 neighbouring positions
- out_weight: bfloat16 [4, 2560, 2560], P('rep', 'fsdp'), may hold values from -0.125 to 0.125
- momentum: float32 [4, 2560, 2560], P('rep', 'fsdp'), may hold values from -192 to 192
- step_index: int32 [1], replicated, may hold values from 0 to 63
Outputs:
- block_out: bfloat16 [4, 3072, 2560], P('rep', 'fsdp')
- query_grad: bfloat16 [4, 3072, 2560], P('rep', 'fsdp')
- key_grad: bfloat16 [4, 3072, 2560], P('rep', 'fsdp')
- value_grad: bfloat16 [4, 3072, 2560], P('rep', 'fsdp')
- new_weight: bfloat16 [4, 2560, 2560], P('rep', 'fsdp')
- new_momentum: float32 [4, 2560, 2560], P('rep', 'fsdp')
All inputs are finite; a program needn't handle non-finite values.
Results may differ from a plain program's by a relative error of at most 0.018.
Values may be sent and summed in bfloat16 or wider, within the bound.
A program may use at most 192 MiB of HBM per device.

v0:
```python
import functools

import jax
import jax.numpy as jnp
from jax import lax
from jax.experimental import pallas as pl
from jax.experimental.pallas import tpu as pltpu
from jax.sharding import PartitionSpec as P

HEAD_SIZE = 128

momentum_decay = 0.9
learning_rate = 0.0003


def swapped(block, axis, distance):
    count = lax.axis_size(axis)
    route = []
    for low in range(count):
        high = low | 1 << distance
        if high != low and high < count:
            route += [(low, high), (high, low)]
    return lax.ppermute(block, axis, route)


def probabilities(q, k, doc_column, doc_row):
    length = q.shape[0]
    scores = lax.dot_general(
        q, k, (((1,), (1,)), ((), ())), preferred_element_type=jnp.float32
    ) * (HEAD_SIZE ** (-0.5))
    rows = lax.broadcasted_iota(jnp.int32, (length, length), 0)
    columns = lax.broadcasted_iota(jnp.int32, (length, length), 1)
    allowed = (columns <= rows) & (doc_column == doc_row)
    scores = jnp.where(allowed, scores, -jnp.inf)
    exponents = jnp.exp(scores - jnp.max(scores, axis=-1, keepdims=True))
    return exponents / jnp.sum(exponents, axis=-1, keepdims=True)


def forward_kernel(q_ref, k_ref, v_ref, doc_column_ref, doc_row_ref, context_ref):
    for head in range(q_ref.shape[1] // HEAD_SIZE):
        cut = slice(head * HEAD_SIZE, (head + 1) * HEAD_SIZE)
        probs = probabilities(q_ref[:, cut], k_ref[:, cut], doc_column_ref[...], doc_row_ref[...])
        context_ref[:, cut] = jnp.dot(
            probs.astype(jnp.bfloat16), v_ref[:, cut], preferred_element_type=jnp.float32
        ).astype(jnp.bfloat16)


def backward_kernel(
    q_ref, k_ref, v_ref, grad_ref, doc_column_ref, doc_row_ref, dq_ref, dk_ref, dv_ref
):
    for head in range(q_ref.shape[1] // HEAD_SIZE):
        cut = slice(head * HEAD_SIZE, (head + 1) * HEAD_SIZE)
        q, k, v, grad = q_ref[:, cut], k_ref[:, cut], v_ref[:, cut], grad_ref[:, cut]
        probs = probabilities(q, k, doc_column_ref[...], doc_row_ref[...])
        dv_ref[:, cut] = lax.dot_general(
            probs.astype(jnp.bfloat16),
            grad,
            (((0,), (0,)), ((), ())),
            preferred_element_type=jnp.float32,
        ).astype(jnp.bfloat16)
        prob_grad = lax.dot_general(
            grad, v, (((1,), (1,)), ((), ())), preferred_element_type=jnp.float32
        )
        row_delta = jnp.sum(prob_grad * probs, axis=-1, keepdims=True)
        score_grad = (probs * (prob_grad - row_delta) * (HEAD_SIZE ** (-0.5))).astype(jnp.bfloat16)
        dq_ref[:, cut] = jnp.dot(score_grad, k, preferred_element_type=jnp.float32).astype(
            jnp.bfloat16
        )
        dk_ref[:, cut] = lax.dot_general(
            score_grad, q, (((0,), (0,)), ((), ())), preferred_element_type=jnp.float32
        ).astype(jnp.bfloat16)


def per_head(kernel, arrays, doc_block, outputs, matmuls):
    length, width = arrays[0].shape
    step = 2 * HEAD_SIZE if width % (2 * HEAD_SIZE) == 0 else HEAD_SIZE
    block = pl.BlockSpec((length, step), lambda h: (0, h))
    whole = lambda shape: pl.BlockSpec(shape, lambda h: (0, 0))
    result = jax.ShapeDtypeStruct((length, width), jnp.bfloat16)
    return pl.pallas_call(
        kernel,
        grid=(width // step,),
        in_specs=[block] * len(arrays) + [whole((length, 1)), whole((1, length))],
        out_specs=[block] * outputs,
        out_shape=[result] * outputs,
        cost_estimate=pl.CostEstimate(
            flops=4 * matmuls * length * length * width,
            bytes_accessed=(len(arrays) + outputs) * length * width * 2,
            transcendentals=length * length * width // HEAD_SIZE,
        ),
    )(*arrays, doc_block[:, None], doc_block[None, :])


def on_device(
    query_rows,
    key_rows,
    value_rows,
    residual_in,
    out_grad,
    doc_ids,
    out_weight,
    momentum,
    step_index,
):
    count = lax.axis_size("fsdp")
    side = lax.axis_index("fsdp") % 2
    groups = [[i for i in range(count) if i % 2 == s] for s in range(2)]
    pair = [(i, i ^ 1) for i in range(count)]
    first = side == 0
    query, key, value = query_rows[0], key_rows[0], value_rows[0]
    weight_shard = out_weight[0]
    own_grad = out_grad[0]
    rows = weight_shard.shape[0]
    gathered = lax.all_gather(
        weight_shard, "fsdp", axis=0, tiled=True, axis_index_groups=groups
    )
    pair_grad = lax.ppermute(own_grad, "fsdp", pair)
    (context,) = per_head(forward_kernel, (query, key, value), doc_ids[0], 1, 2)

    def half(array, which):
        return jnp.concatenate(
            [array[:, j * rows : (j + 1) * rows] for j in range(which, count, 2)], axis=1
        )

    low, high = half(context, 0), half(context, 1)
    own_context = jnp.where(first, low, high)
    pair_context = lax.ppermute(jnp.where(first, high, low), "fsdp", pair)

    def outer(left, right):
        return lax.dot_general(
            left, right, (((0,), (0,)), ((), ())), preferred_element_type=jnp.float32
        )

    weight_term = (outer(own_context, own_grad) + outer(pair_context, pair_grad)).astype(
        jnp.bfloat16
    )
    weight_grad = lax.psum_scatter(
        weight_term, "fsdp", scatter_dimension=0, tiled=True, axis_index_groups=groups
    ).astype(jnp.float32)

    def back(grad):
        return lax.dot_general(
            grad, gathered, (((1,), (1,)), ((), ())), preferred_element_type=jnp.float32
        ).astype(jnp.bfloat16)

    got_back = lax.ppermute(back(pair_grad), "fsdp", pair)
    pair_out = jnp.dot(pair_context, gathered, preferred_element_type=jnp.float32)
    got_out = lax.ppermute(pair_out.astype(jnp.bfloat16), "fsdp", pair)
    own_back = back(own_grad)
    even = jnp.where(first, own_back, got_back)
    odd = jnp.where(first, got_back, own_back)
    pieces = []
    for j in range(count // 2):
        cut = slice(j * rows, (j + 1) * rows)
        pieces += [even[:, cut], odd[:, cut]]
    context_grad = jnp.concatenate(pieces, axis=1)
    query_grad, key_grad, value_grad = per_head(
        backward_kernel, (query, key, value, context_grad), doc_ids[0], 3, 5
    )
    own_out = jnp.dot(own_context, gathered, preferred_element_type=jnp.float32)
    block_out = (
        residual_in[0].astype(jnp.float32) + own_out + got_out.astype(jnp.float32)
    ).astype(jnp.bfloat16)

    new_momentum = momentum_decay * momentum[0] + weight_grad
    stepped = (weight_shard.astype(jnp.float32) - learning_rate * new_momentum).astype(jnp.bfloat16)
    levels = lax.axis_size("rep").bit_length() - 1
    branches = [functools.partial(swapped, axis="rep", distance=level) for level in range(levels)]
    partner = lax.switch(step_index[0] % levels, branches, stepped)
    new_weight = ((stepped.astype(jnp.float32) + partner.astype(jnp.float32)) * 0.5).astype(
        jnp.bfloat16
    )
    return (
        block_out[None],
        query_grad[None],
        key_grad[None],
        value_grad[None],
        new_weight[None],
        new_momentum[None],
    )


def solution(mesh):
    rows = P("rep", "fsdp", None)
    return jax.shard_map(
        on_device,
        mesh=mesh,
        in_specs=(rows, rows, rows, rows, rows, P("rep", "fsdp"), rows, rows, P()),
        out_specs=(rows,) * 6,
        check_vma=False,
    )
```

profile of v0, /device:TPU:0, one launch (start us, length us, event | category | flops | bytes accessed | tf_op | source)
XLA Modules:
  0.0 265.9 jit_solution(17441154624036472439)
XLA Ops:
  7.9 3.0 %collective-permute-start.4 = (bf16[384,2560]{1,0:T(8,128)(2,1)}, bf16[384,2560]{1,0:T(8,128)(2,1)}, u32[]{:S(2)}, u32[]{:S(2)}) collective-permute-start(bf16[384,2560]{1,0:T(8,128)(2,1)} %bitcast.55), channel_id=1, source_target_pairs={{0,1},{1,0},{2,3},{3,2},{4,5},{5,4},{6,7},{7,6},{8,9},{9,8},{10,11... | collective-permute-start | bytes 5898248 | tf_op jit(solution)/shard_map/ppermute | solution.py:117
  11.0 1.5 copy.15.doc_column_ref
  12.5 14.1 %shard_map.136 = bf16[384,2560]{1,0:T(8,128)(2,1)} custom-call(bf16[384,2560]{1,0:T(8,128)(2,1)} %bitcast.57, bf16[384,2560]{1,0:T(8,128)(2,1)} %bitcast.59, bf16[384,2560]{1,0:T(8,128)(2,1)} %bitcast.61, s32[384,1]{1,0:T(8,128)} %copy.15.doc_column_ref, s32[1,384]{1,0:T(1,128)} %doc_row_ref.3), custom_call_target="tpu_custom_call" | custom-call | flops 3019898880 | bytes 7864320 | tf_op jit(solution)/shard_map/pallas_call | solution.py:80
  26.6 2.2 fusion.28
  30.4 1.3 copy-done.1
  31.8 3.6 %fusion.25 = f32[1280,2560]{1,0:T(8,128)S(1)} fusion(bf16[384,1280]{1,0:T(8,128)(2,1)S(1)} %concatenate.9, bf16[384,1280]{1,0:T(8,128)(2,1)S(1)} %concatenate.10, pred[]{:T(512)S(6)} %eq.6, bf16[1,384,2560]{2,1,0:T(8,128)(2,1)S(1)} %copy-done.1), kind=kOutput, calls=%fused_computation.26 | convolution fusion | flops 2517073920 | bytes 17039360 | tf_op jit(solution)/shard_map/dot_general | solution.py:130
  35.4 39.7 %collective-permute-done.2 = bf16[384,1280]{1,0:T(8,128)(2,1)S(1)} collective-permute-done((bf16[384,1280]{1,0:T(8,128)(2,1)S(1)}, bf16[384,1280]{1,0:T(8,128)(2,1)S(1)}, u32[]{:S(2)}, u32[]{:S(2)}) %collective-permute-start.2) | collective-permute-done | bytes 983072 | tf_op jit(solution)/shard_map/ppermute | solution.py:127
  75.1 7.4 %fusion = bf16[1280,2560]{1,0:T(8,128)(2,1)} fusion(f32[1280,2560]{1,0:T(8,128)S(1)} %fusion.25, bf16[384,1280]{1,0:T(8,128)(2,1)S(1)} %collective-permute-done.2, bf16[384,2560]{1,0:T(8,128)(2,1)} %collective-permute-done.4), kind=kOutput, calls=%fused_computation.1 | convolution fusion | flops 2523136000 | bytes 22609920 | tf_op jit(solution)/shard_map/dot_general | solution.py:130
  83.2 48.7 %all-gather.3.cloned.1.call-done = bf16[1,1280,2560]{2,1,0:T(8,128)(2,1)} async-done(((bf16[1,320,2560]{2,1,0:T(8,128)(2,1)}), bf16[1,1280,2560]{2,1,0:T(8,128)(2,1)}) %all-gather.3.cloned.1.call-update) | async-done | bytes 6553616 | tf_op jit(solution)/shard_map/all_gather | solution.py:114
  131.9 6.3 %fusion.19 = bf16[384,1280]{1,0:T(8,128)(2,1)S(1)} fusion(bf16[384,2560]{1,0:T(8,128)(2,1)} %collective-permute-done.4, bf16[1,1280,2560]{2,1,0:T(8,128)(2,1)} %all-gather.3.cloned.1.call-done), kind=kOutput, calls=%fused_computation.18 | convolution fusion | flops 2517073920 | bytes 9502720 | tf_op jit(solution)/shard_map/dot_general | solution.py:142
  138.3 1.5 collective-permute-start.5
  139.8 3.8 %fusion.12 = bf16[384,2560]{1,0:T(8,128)(2,1)} fusion(bf16[384,1280]{1,0:T(8,128)(2,1)S(1)} %collective-permute-done.2, bf16[1,1280,2560]{2,1,0:T(8,128)(2,1)S(1)} %copy-done.3), kind=kOutput, calls=%fused_computation.11 | convolution fusion | flops 2517565440 | bytes 9502720 | tf_op jit(solution)/shard_map/dot_general | solution.py:147
  144.2 4.7 %fusion.9 = f32[384,2560]{1,0:T(8,128)} fusion(bf16[1,1280,2560]{2,1,0:T(8,128)(2,1)S(1)} %copy-done.3, bf16[1,384,2560]{2,1,0:T(8,128)(2,1)S(1)} %copy-done.4, bf16[384,1280]{1,0:T(8,128)(2,1)S(1)} %concatenate.9, bf16[384,1280]{1,0:T(8,128)(2,1)S(1)} %concatenate.10, pred[]{:T(512)S(6)} %eq.6), kind=kOutput, calls=%fused_computation.10 | convolution fusion | flops 2519040000 | bytes 14417921 | tf_op jit(solution)/shard_map/dot_general | solution.py:160
  148.9 2.7 %fusion.16 = bf16[384,1280]{1,0:T(8,128)(2,1)S(1)} fusion(bf16[1,1280,2560]{2,1,0:T(8,128)(2,1)S(1)} %copy-done.3, bf16[1,384,2560]{2,1,0:T(8,128)(2,1)S(1)} %copy-done.2), kind=kOutput, calls=%fused_computation.17 | convolution fusion | flops 2517073920 | bytes 9502720 | tf_op jit(solution)/shard_map/dot_general | solution.py:142
  151.6 11.4 %collective-permute-done.5 = bf16[384,1280]{1,0:T(8,128)(2,1)S(1)} collective-permute-done((bf16[384,1280]{1,0:T(8,128)(2,1)S(1)}, bf16[384,1280]{1,0:T(8,128)(2,1)S(1)}, u32[]{:S(2)}, u32[]{:S(2)}) %collective-permute-start.5) | collective-permute-done | bytes 983072 | tf_op jit(solution)/shard_map/ppermute | solution.py:146
  163.7 4.0 %concatenate.11.grad_ref = bf16[384,2560]{1,0:T(8,128)(2,1)} concatenate(bf16[384,320]{1,0:T(8,128)(2,1)S(1)} %get-tuple-element.43, bf16[384,320]{1,0:T(8,128)(2,1)S(1)} %get-tuple-element.38, bf16[384,320]{1,0:T(8,128)(2,1)S(1)} %get-tuple-element.44, bf16[384,320]{1,0:T(8,128)(2,1)S(1)} %get-tuple-element.37, bf16[384,320]{1,0:T(8,128)(2,1)S(1)} %get-tuple-element.45, ...), dimensions={1} | concatenate | bytes 3932160 | tf_op jit(solution)/shard_map/concatenate | solution.py:156
  167.7 22.9 %shard_map.137 = (bf16[384,2560]{1,0:T(8,128)(2,1)}, bf16[384,2560]{1,0:T(8,128)(2,1)}, bf16[384,2560]{1,0:T(8,128)(2,1)}) custom-call(bf16[384,2560]{1,0:T(8,128)(2,1)} %bitcast.58, bf16[384,2560]{1,0:T(8,128)(2,1)} %bitcast.60, bf16[384,2560]{1,0:T(8,128)(2,1)} %bitcast.62, bf16[384,2560]{1,0:T(8,128)(2,1)} %concatenate.11.grad_ref, ...), custom_call_target="tpu_custom_call" | custom-call | flops 7549747200 | bytes 13762560 | tf_op jit(solution)/shard_map/pallas_call | solution.py:80
  190.6 13.7 %collective-permute-done.3 = bf16[384,2560]{1,0:T(8,128)(2,1)} collective-permute-done((bf16[384,2560]{1,0:T(8,128)(2,1)}, bf16[384,2560]{1,0:T(8,128)(2,1)}, u32[]{:S(2)}, u32[]{:S(2)}) %collective-permute-start.3) | collective-permute-done | bytes 1966112 | tf_op jit(solution)/shard_map/ppermute | solution.py:148
  204.2 4.5 %fusion.23 = bf16[1,384,2560]{2,1,0:T(8,128)(2,1)} fusion(f32[384,2560]{1,0:T(8,128)} %fusion.9, bf16[384,2560]{1,0:T(8,128)(2,1)} %collective-permute-done.3), kind=kLoop, calls=%fused_computation.20 | loop fusion | flops 2949120 | bytes 7864320 | tf_op jit(solution)/shard_map/broadcast_in_dim | solution.py:174
  208.8 38.7 %reduce-scatter.2.cloned.1.call-done = bf16[320,2560]{1,0:T(8,128)(2,1)} async-done(((bf16[1280,2560]{1,0:T(8,128)(2,1)}), bf16[320,2560]{1,0:T(8,128)(2,1)}) %reduce-scatter.2.cloned.1.call-update) | async-done | bytes 1638416 | tf_op jit(solution)/shard_map/reduce_scatter | solution.py:137
  247.5 4.9 %fusion.22 = (f32[1,320,2560]{2,1,0:T(8,128)}, bf16[320,2560]{1,0:T(8,128)(2,1)S(1)}) fusion(bf16[320,2560]{1,0:T(8,128)(2,1)} %reduce-scatter.2.cloned.1.call-done, f32[1,320,2560]{2,1,0:T(8,128)} %param.18, bf16[1,320,2560]{2,1,0:T(8,128)(2,1)S(1)} %copy-done), kind=kLoop, calls=%fused_computation.19 | loop fusion | flops 5734400 | bytes 11468800 | tf_op jit(solution)/shard_map/broadcast_in_dim | solution.py:179
  252.3 3.6 %conditional.4 = (bf16[320,2560]{1,0:T(8,128)(2,1)}) conditional(s32[]{:T(128)} %clamp.3, bf16[320,2560]{1,0:T(8,128)(2,1)S(1)} %get-tuple-element.24, bf16[320,2560]{1,0:T(8,128)(2,1)S(1)} %get-tuple-element.24), branch_computations={%region_1.2_spmd, %region_2.3_spmd} | conditional | bytes 6553648
  252.3 3.6 %collective-permute-done = bf16[320,2560]{1,0:T(8,128)(2,1)} collective-permute-done((bf16[320,2560]{1,0:T(8,128)(2,1)S(1)}, bf16[320,2560]{1,0:T(8,128)(2,1)}, u32[]{:S(2)}, u32[]{:S(2)}) %collective-permute-start) | collective-permute-done | bytes 1638432 | tf_op jit(solution)/shard_map/cond/branch_0_fun/ppermute | solution.py:23
  256.0 3.1 %fusion.24 = bf16[1,320,2560]{2,1,0:T(8,128)(2,1)} fusion(bf16[320,2560]{1,0:T(8,128)(2,1)} %get-tuple-element.47, bf16[320,2560]{1,0:T(8,128)(2,1)S(1)} %get-tuple-element.24), kind=kLoop, calls=%fused_computation.21 | loop fusion | flops 4096000 | bytes 4915200 | tf_op jit(solution)/shard_map/broadcast_in_dim | solution.py:178
  (22 shorter events, 3.7 us)
Async XLA Ops:
  7.2 124.8 %all-gather.3.cloned.1.call-start = ((), (), s32[]{:S(2)}) async-start(), calls=%async_computation.2 | async-start | bytes 8192000 | tf_op jit(solution)/shard_map/all_gather | solution.py:114
  7.9 239.6 %reduce-scatter.2.cloned.1.call-start = ((), (), s32[]{:S(2)}) async-start(), calls=%async_computation.1 | async-start | bytes 8192000 | tf_op jit(solution)/shard_map/reduce_scatter | solution.py:137
  7.9 67.1 %collective-permute-start.4 = (bf16[384,2560]{1,0:T(8,128)(2,1)}, bf16[384,2560]{1,0:T(8,128)(2,1)}, u32[]{:S(2)}, u32[]{:S(2)}) collective-permute-start(bf16[384,2560]{1,0:T(8,128)(2,1)} %bitcast.55), channel_id=1, source_target_pairs={{0,1},{1,0},{2,3},{3,2},{4,5},{5,4},{6,7},{7,6},{8,9},{9,8},{10,11... | collective-permute-start | bytes 5898248 | tf_op jit(solution)/shard_map/ppermute | solution.py:117
  30.2 1.6 copy-start.1
  30.3 44.7 %collective-permute-start.2 = (bf16[384,1280]{1,0:T(8,128)(2,1)S(1)}, bf16[384,1280]{1,0:T(8,128)(2,1)S(1)}, u32[]{:S(2)}, u32[]{:S(2)}) collective-permute-start(bf16[384,1280]{1,0:T(8,128)(2,1)S(1)} %broadcast_select_fusion.2), channel_id=1, source_target_pairs={{0,1},{1,0},{2,3},{3,2},{4,5},{5,4},{6,7},{7,6},{8,9},{9,8},{10,11... | collective-permute-start | bytes 2949128 | tf_op jit(solution)/shard_map/ppermute | solution.py:127
  131.9 7.9 %copy-start.3 = (bf16[1,1280,2560]{2,1,0:T(8,128)(2,1)S(1)}, bf16[1,1280,2560]{2,1,0:T(8,128)(2,1)}, u32[]{:S(2)}) copy-start(bf16[1,1280,2560]{2,1,0:T(8,128)(2,1)} %all-gather.3.cloned.1.call-done) | copy-start | bytes 19660804
  138.3 6.0 %copy-start.4 = (bf16[1,384,2560]{2,1,0:T(8,128)(2,1)S(1)}, bf16[1,384,2560]{2,1,0:T(8,128)(2,1)}, u32[]{:S(2)}) copy-start(bf16[1,384,2560]{2,1,0:T(8,128)(2,1)} %param.14) | copy-start | bytes 5898244
  138.3 24.7 %collective-permute-start.5 = (bf16[384,1280]{1,0:T(8,128)(2,1)S(1)}, bf16[384,1280]{1,0:T(8,128)(2,1)S(1)}, u32[]{:S(2)}, u32[]{:S(2)}) collective-permute-start(bf16[384,1280]{1,0:T(8,128)(2,1)S(1)} %fusion.19), channel_id=1, source_target_pairs={{0,1},{1,0},{2,3},{3,2},{4,5},{5,4},{6,7},{7,6},{8,9},{9,8},{10,11... | collective-permute-start | bytes 2949128 | tf_op jit(solution)/shard_map/ppermute | solution.py:146
  143.6 5.2 %copy-start.2 = (bf16[1,384,2560]{2,1,0:T(8,128)(2,1)S(1)}, bf16[1,384,2560]{2,1,0:T(8,128)(2,1)}, u32[]{:S(2)}) copy-start(bf16[1,384,2560]{2,1,0:T(8,128)(2,1)} %param.15) | copy-start | bytes 5898244
  143.6 60.6 %collective-permute-start.3 = (bf16[384,2560]{1,0:T(8,128)(2,1)}, bf16[384,2560]{1,0:T(8,128)(2,1)}, u32[]{:S(2)}, u32[]{:S(2)}) collective-permute-start(bf16[384,2560]{1,0:T(8,128)(2,1)} %fusion.12), channel_id=1, source_target_pairs={{0,1},{1,0},{2,3},{3,2},{4,5},{5,4},{6,7},{7,6},{8,9},{9,8},{10,11... | collective-permute-start | bytes 5898248 | tf_op jit(solution)/shard_map/ppermute | solution.py:148
  190.6 56.9 %copy-start = (bf16[1,320,2560]{2,1,0:T(8,128)(2,1)S(1)}, bf16[1,320,2560]{2,1,0:T(8,128)(2,1)}, u32[]{:S(2)}) copy-start(bf16[1,320,2560]{2,1,0:T(8,128)(2,1)} %param.17) | copy-start | bytes 4915204
  252.3 3.6 %collective-permute-start = (bf16[320,2560]{1,0:T(8,128)(2,1)S(1)}, bf16[320,2560]{1,0:T(8,128)(2,1)}, u32[]{:S(2)}, u32[]{:S(2)}) collective-permute-start(bf16[320,2560]{1,0:T(8,128)(2,1)S(1)} %param), channel_id=1, source_target_pairs={{0,8},{8,0},{16,24},{24,16},{1,9},{9,1},{17,25},{25,17},{2,10},{10... | collective-permute-start | bytes 4915208 | tf_op jit(solution)/shard_map/cond/branch_0_fun/ppermute | solution.py:23
Sparse Core Ops, SparseCore 0:
  9.5 122.3 all-gather.2
  134.2 113.1 reduce-scatter.1
where the time goes:
time: 266 us
  waiting for transfers between devices  156 us (59%)
  Pallas kernels  37 us (14%)
  matrix products  28.6 us (11%)
  between operations  14.8 us (6%)
  other arithmetic  12.7 us (5%)
  local copies, waits for them, and re-layouts  11.1 us (4%)
  starting transfers between devices  5.3 us (2%)
    all_gather x1, waiting for transfers between devices, on_device(): lax.all_gather(weight_shard, 'fsdp', axis=0, tiled=True, axis_index_group...  48.7 us
    ppermute x1, waiting for transfers between devices, on_device(): pair_context = lax.ppermute(jnp.where(first, high, low), 'fsdp', pair)  39.7 us
    reduce_scatter x1, waiting for transfers between devices, on_device(): lax.psum_scatter(weight_term, 'fsdp', scatter_dimension=0, tiled=True, ax...  38.7 us
    pallas_call x2, Pallas kernels, per_head(): pl.pallas_call(kernel, grid=(width // step,), in_specs=[block] * len(arra...  37 us
    ppermute x1, waiting for transfers between devices, on_device(): got_out = lax.ppermute(pair_out.astype(jnp.bfloat16), 'fsdp', pair)  13.7 us
    ppermute x1, waiting for transfers between devices, on_device(): got_back = lax.ppermute(back(pair_grad), 'fsdp', pair)  11.4 us
    dot_general x2, matrix products, outer(): lax.dot_general(left, right, (((0,), (0,)), ((), ())), preferred_element_...  11 us
    dot_general x2, matrix products, back(): lax.dot_general(grad, gathered, (((1,), (1,)), ((), ())), preferred_eleme...  9.04 us
  transfers between devices with their start and end apart: 7, of which 6 were waited for; matrix products, arithmetic and copies ran while one was open for 16% of the time, Pallas kernels for 14%

commit v1 on v0

--- a/solution.py
+++ b/solution.py
@@ -91,6 +91,590 @@
     )(*arrays, doc_block[:, None], doc_block[None, :])
 
 
+MESH = pl.DeviceIdType.MESH
+LANES = 128
+
+
+def dot(a, b, ca, cb):
+    return lax.dot_general(
+        a, b, (((ca,), (cb,)), ((), ())), preferred_element_type=jnp.float32
+    )
+
+
+def line_kernel(
+    n,
+    levels,
+    q_hbm,
+    k_hbm,
+    v_hbm,
+    res_hbm,
+    g_hbm,
+    w_hbm,
+    mom_hbm,
+    doc_ref,
+    step_ref,
+    out_hbm,
+    dq_hbm,
+    dk_hbm,
+    dv_hbm,
+    nw_hbm,
+    nm_hbm,
+    wbuf,
+    gown,
+    gpair,
+    qb,
+    kb,
+    vb,
+    ctx,
+    ctxp,
+    cg,
+    cgs,
+    acc,
+    oacc,
+    osend,
+    ogot,
+    rs,
+    mb,
+    st,
+    pr,
+    rb,
+    bias,
+    hs,
+    ws,
+    gs,
+    ms,
+    ys,
+    ns,
+    xg_s,
+    xg_r,
+    xc_s,
+    xc_r,
+    xb_s,
+    xb_r,
+    xo_s,
+    xo_r,
+    zs,
+    zr,
+    ps,
+    pr_r,
+):
+    units, chunks, rows, wide = wbuf.shape
+    heads, tokens, size = qb.shape
+    per = heads // n
+    scale = HEAD_SIZE ** (-0.5)
+    me = lax.axis_index("fsdp")
+    rep = lax.axis_index("rep")
+    z = lax.div(me, 2)
+    x = lax.rem(me, 2)
+    pair = me + 1 - 2 * x
+    at_end = (z == 0) | (z == n - 1)
+
+    def partner(level):
+        bit = lax.rem(lax.div(rep, 1 << level), 2)
+        return rep + (1 << level) - (2 << level) * bit
+
+    def lanes(c, width):
+        return pl.ds(pl.multiple_of(c * width, width), width)
+
+    def own_rows(u):
+        return pl.ds(pl.multiple_of((2 * u + x) * rows, 16), rows)
+
+    def pair_rows(u):
+        return pl.ds(pl.multiple_of((2 * u + 1 - x) * rows, 16), rows)
+
+    def head_rows(h):
+        return pl.ds(pl.multiple_of(h * size, size), size)
+
+    def load_head(i, h):
+        src = (q_hbm, k_hbm, v_hbm)[i]
+        dst = (qb, kb, vb)[i]
+        return pltpu.make_async_copy(src.at[:, lanes(h, size)], dst.at[h], hs.at[i, h])
+
+    def store_head(i, h):
+        src = (qb, kb, vb)[i]
+        dst = (dq_hbm, dk_hbm, dv_hbm)[i]
+        return pltpu.make_async_copy(src.at[h], dst.at[:, lanes(h, size)], hs.at[i, h])
+
+    def load_w(c):
+        return pltpu.make_async_copy(w_hbm.at[:, lanes(c, wide)], wbuf.at[z, c], ws.at[c])
+
+    def load_g(c):
+        return pltpu.make_async_copy(g_hbm.at[:, lanes(c, wide)], gown.at[c], gs.at[c])
+
+    def load_m(c):
+        return pltpu.make_async_copy(mom_hbm.at[:, lanes(c, wide)], mb.at[c], ms.at[c])
+
+    def store_m(c):
+        return pltpu.make_async_copy(mb.at[c], nm_hbm.at[:, lanes(c, wide)], ms.at[c])
+
+    def load_y(c):
+        return pltpu.make_async_copy(res_hbm.at[:, lanes(c, wide)], rb.at[c], ys.at[c])
+
+    def store_y(c):
+        return pltpu.make_async_copy(rb.at[c], out_hbm.at[:, lanes(c, wide)], ys.at[c])
+
+    def store_n(c):
+        return pltpu.make_async_copy(pr.at[0, c], nw_hbm.at[:, lanes(c, wide)], ns.at[c])
+
+    def to_pair(src, dst, send, recv):
+        return pltpu.make_async_remote_copy(
+            src_ref=src,
+            dst_ref=dst,
+            send_sem=send,
+            recv_sem=recv,
+            device_id={"fsdp": pair},
+            device_id_type=MESH,
+        )
+
+    def x_grad(c):
+        return to_pair(g_hbm.at[:, lanes(c, wide)], gpair.at[c], xg_s.at[c], xg_r.at[c])
+
+    def x_context(u):
+        return to_pair(ctx.at[pair_rows(u), :], ctxp.at[u], xc_s.at[u], xc_r.at[u])
+
+    def x_back(u):
+        return to_pair(cgs.at[u], cg.at[own_rows(u), :], xb_s.at[u], xb_r.at[u])
+
+    def x_out(c):
+        return to_pair(osend.at[c], ogot.at[c], xo_s.at[c], xo_r.at[c])
+
+    def along(d, p, c, src, dst):
+        return pltpu.make_async_remote_copy(
+            src_ref=src,
+            dst_ref=dst,
+            send_sem=zs.at[d, p - 1, c],
+            recv_sem=zr.at[d, p - 1, c],
+            device_id={"fsdp": me + 2 - 4 * d},
+            device_id_type=MESH,
+        )
+
+    def place(d):
+        return z + d * (n - 1 - 2 * z)
+
+    def swap(level, c):
+        return pltpu.make_async_remote_copy(
+            src_ref=st.at[c],
+            dst_ref=pr.at[level, c],
+            send_sem=ps.at[level, c],
+            recv_sem=pr_r.at[level, c],
+            device_id={"rep": partner(level)},
+            device_id_type=MESH,
+        )
+
+    def block_at(i):
+        return jnp.where(2 * z < n, n - 1 - i, i)
+
+    def each(count, body):
+        def run(i, carry):
+            body(i)
+            return carry
+
+        lax.fori_loop(0, count, run, 0)
+
+    def start_loads(i):
+        u = block_at(i)
+
+        def one(hh):
+            for a in range(3):
+                load_head(a, u * per + hh).start()
+
+        each(per, one)
+
+    start_loads(0)
+
+    barrier = pltpu.get_barrier_semaphore()
+    pl.semaphore_signal(barrier, inc=1, device_id={"fsdp": pair}, device_id_type=MESH)
+    for level in range(levels):
+        pl.semaphore_signal(
+            barrier, inc=1, device_id={"rep": partner(level)}, device_id_type=MESH
+        )
+
+    @pl.when(z > 0)
+    def _():
+        pl.semaphore_signal(barrier, inc=1, device_id={"fsdp": me - 2}, device_id_type=MESH)
+
+    @pl.when(z < n - 1)
+    def _():
+        pl.semaphore_signal(barrier, inc=1, device_id={"fsdp": me + 2}, device_id_type=MESH)
+
+    pl.semaphore_wait(barrier, 1 + levels + jnp.where(at_end, 1, 2))
+
+    def first_sends(c):
+        def one(d):
+            @pl.when(place(d) < n - 1)
+            def _():
+                along(d, 1, c, w_hbm.at[:, lanes(c, wide)], wbuf.at[z, c]).start()
+
+        each(2, one)
+
+    each(chunks, first_sends)
+    x_grad(0).start()
+    each(n - 1, lambda i: start_loads(i + 1))
+
+    def other_loads(c):
+        load_g(c).start()
+        load_w(c).start()
+        load_m(c).start()
+        load_y(c).start()
+
+    each(chunks, other_loads)
+
+    row_ids = jnp.broadcast_to(doc_ref[...], (tokens, tokens))
+    column_ids = jnp.transpose(row_ids)
+    r = lax.broadcasted_iota(jnp.int32, (tokens, tokens), 0)
+    s = lax.broadcasted_iota(jnp.int32, (tokens, tokens), 1)
+    bias[...] = jnp.where((s <= r) & (row_ids == column_ids), 0.0, -jnp.inf)
+
+    blocks = tokens // LANES
+
+    def probabilities_of(q, k, i):
+        seen = (i + 1) * LANES
+        scores = dot(q[i * LANES : seen], k[:seen], 1, 1) * scale
+        scores = scores + bias[i * LANES : seen, :seen]
+        exponents = jnp.exp(scores - jnp.max(scores, axis=-1, keepdims=True))
+        return exponents * (1.0 / jnp.sum(exponents, axis=-1, keepdims=True))
+
+    def forward_head(h):
+        q, k, v = qb[h], kb[h], vb[h]
+        parts = []
+        for i in range(blocks):
+            probs = probabilities_of(q, k, i).astype(jnp.bfloat16)
+            parts.append(dot(probs, v[: (i + 1) * LANES], 1, 0))
+        context = jnp.concatenate(parts, axis=0)
+        ctx[head_rows(h), :] = jnp.transpose(context).astype(jnp.bfloat16)
+
+    def forward_block(i):
+        u = block_at(i)
+
+        def one(hh):
+            h = u * per + hh
+            for a in range(3):
+                load_head(a, h).wait()
+            forward_head(h)
+
+        each(per, one)
+        x_context(u).start()
+
+        @pl.when(i == 0)
+        def _():
+            each(chunks - 1, lambda c: x_grad(c + 1).start())
+
+    each(n, forward_block)
+
+    def wait_loads(c):
+        load_g(c).wait()
+        load_w(c).wait()
+        load_m(c).wait()
+        load_y(c).wait()
+
+    each(chunks, wait_loads)
+
+    def backward_head(h):
+        q, k, v = qb[h], kb[h], vb[h]
+        grad = jnp.transpose(cg[head_rows(h), :].astype(jnp.float32)).astype(jnp.bfloat16)
+        low, score_grads, parts = [], [], []
+        for i in range(blocks):
+            seen = (i + 1) * LANES
+            probs = probabilities_of(q, k, i)
+            low.append(probs.astype(jnp.bfloat16))
+            prob_grad = dot(grad[i * LANES : seen], v[:seen], 1, 1)
+            row_delta = jnp.sum(prob_grad * probs, axis=-1, keepdims=True)
+            score_grad = (probs * (prob_grad - row_delta) * scale).astype(jnp.bfloat16)
+            score_grads.append(score_grad)
+            parts.append(dot(score_grad, k[:seen], 1, 0))
+        for i in range(blocks):
+            cut = slice(i * LANES, (i + 1) * LANES)
+            qb[h, cut, :] = parts[i].astype(jnp.bfloat16)
+        for j in range(blocks):
+            cut = slice(j * LANES, (j + 1) * LANES)
+            scores_j = jnp.concatenate([b[:, cut] for b in score_grads[j:]], axis=0)
+            probs_j = jnp.concatenate([b[:, cut] for b in low[j:]], axis=0)
+            kb[h, cut, :] = dot(scores_j, q[j * LANES :], 0, 0).astype(jnp.bfloat16)
+            vb[h, cut, :] = dot(probs_j, grad[j * LANES :], 0, 0).astype(jnp.bfloat16)
+
+    def backward_unit(u):
+        x_back(u).wait_recv()
+
+        def one(hh):
+            h = u * per + hh
+            backward_head(h)
+            for a in range(3):
+                store_head(a, h).start()
+
+        each(per, one)
+
+    def weight_part(u, c):
+        return dot(ctx[own_rows(u), :], gown[c], 1, 0) + dot(ctxp[u], gpair[c], 1, 0)
+
+    def unit_chunk(u, c):
+        weight = wbuf[u, c]
+        for side in range(2):
+            left = ctx[own_rows(u), :] if side == 0 else ctxp[u]
+            grad = gown[c] if side == 0 else gpair[c]
+            before = jnp.where(u == z, 0.0, oacc[side, c])
+            oacc[side, c] = before + dot(left, weight, 0, 0)
+            before = jnp.where(c == 0, 0.0, acc[side])
+            acc[side] = before + dot(weight, grad, 1, 1)
+
+        @pl.when(c == chunks - 1)
+        def _():
+            cgs[u] = acc[1].astype(jnp.bfloat16)
+            cg[own_rows(u), :] = acc[0].astype(jnp.bfloat16)
+            x_back(u).start()
+
+    far = jnp.where(2 * z < n, z + 2, z - 2)
+
+    def finish(c):
+        total = weight_part(z, c)
+        total = total + jnp.where(z > 0, rs[z, c].astype(jnp.float32), 0.0)
+        total = total + jnp.where(z < n - 1, rs[n, c].astype(jnp.float32), 0.0)
+        moment = momentum_decay * mb[c] + total
+        mb[c] = moment
+        stepped = wbuf[z, c].astype(jnp.float32) - learning_rate * moment
+        st[c] = stepped.astype(jnp.bfloat16)
+        store_m(c).start()
+        for level in range(levels):
+            swap(level, c).start()
+        x_out(c).wait_recv()
+        total_out = rb[c].astype(jnp.float32) + oacc[0, c] + ogot[c].astype(jnp.float32)
+        rb[c] = total_out.astype(jnp.bfloat16)
+        store_y(c).start()
+
+    def average(c):
+        for level in range(levels):
+            swap(level, c).wait_recv()
+        level_now = jnp.full((rows, wide), lax.rem(step_ref[0], levels), jnp.int32)
+        other = pr[levels - 1, c].astype(jnp.float32)
+        for level in range(levels - 1):
+            other = jnp.where(level_now == level, pr[level, c].astype(jnp.float32), other)
+        mean = (st[c].astype(jnp.float32) + other) * 0.5
+        pr[0, c] = mean.astype(jnp.bfloat16)
+        store_n(c).start()
+
+    def step(t):
+        p = 2 + lax.div(t, chunks)
+        c = lax.rem(t, chunks)
+
+        @pl.when(p <= n + 1)
+        def _():
+            def arrived(d):
+                @pl.when(place(d) > 0)
+                def _():
+                    along(d, p - 1, c, rs.at[0, 0], rs.at[0, 0]).wait_recv()
+
+            each(2, arrived)
+
+        @pl.when(p <= n)
+        def _():
+            def forward(d):
+                zz = place(d)
+
+                @pl.when((zz < n - 1) & (p <= zz + 1))
+                def _():
+                    u = zz + 1 - p
+                    u = u + d * (n - 1 - 2 * u)
+                    along(d, p, c, wbuf.at[u, c], wbuf.at[u, c]).start()
+
+            each(2, forward)
+
+            @pl.when(p == 2)
+            def _():
+                x_grad(c).wait_recv()
+
+                @pl.when(c == 0)
+                def _():
+                    x_context(block_at(0)).wait_recv()
+
+            @pl.when((p == 3) & (c == 0))
+            def _():
+                each(n - 1, lambda i: x_context(block_at(i + 1)).wait_recv())
+
+            def reduce(d):
+                zz = place(d)
+
+                @pl.when((zz < n - 1) & (p > zz + 1))
+                def _():
+                    b = zz + 1 + n - p
+                    b = b + d * (n - 1 - 2 * b)
+                    before = jnp.where(zz > 0, rs[b, c].astype(jnp.float32), 0.0)
+                    rs[b, c] = (before + weight_part(b, c)).astype(jnp.bfloat16)
+                    slot = jnp.where((p == n) & (d == 1), n, b)
+                    along(d, p, c, rs.at[b, c], rs.at[slot, c]).start()
+
+            each(2, reduce)
+
+        @pl.when(p == n + 1)
+        def _():
+            finish(c)
+
+        @pl.when(t >= (n - 1) * chunks + 1)
+        def _():
+            average(t - ((n - 1) * chunks + 1))
+
+        @pl.when((p == 3) | (p == 4))
+        def _():
+            def unit(i):
+                whole = jnp.where(
+                    p == 3,
+                    jnp.where(c == 0, z, jnp.where(c == 1, z - 1, jnp.where(c == 2, z + 1, -1))),
+                    jnp.where(c == 0, far, -1),
+                )
+                single = jnp.where((p == n) & at_end, n - 1 - z, -1)
+                u = jnp.where(i == 0, whole, single)
+                low = jnp.where(i == 0, 0, c)
+                high = jnp.where(i == 0, chunks, c + 1)
+
+                @pl.when((u >= 0) & (u < n))
+                def _():
+                    def one(cc, carry):
+                        unit_chunk(u, cc)
+                        return carry
+
+                    lax.fori_loop(low, high, one, 0)
+
+            each(2, unit)
+
+        @pl.when(p == n)
+        def _():
+            osend[c] = oacc[1, c].astype(jnp.bfloat16)
+            x_out(c).start()
+
+        last = jnp.where(at_end, n - 1 - z, -1)
+        back = jnp.where(
+            p == 4,
+            jnp.where(c == 1, z, jnp.where(c == 2, z - 1, jnp.where(c == 3, z + 1, -1))),
+            jnp.where(p == 5, jnp.where(c == 0, far, jnp.where(c == chunks - 2, last, -1)), -1),
+        )
+
+        @pl.when((back >= 0) & (back < n))
+        def _():
+            backward_unit(back)
+
+    each(n * chunks + 1, step)
+
+    def ends(c):
+        def line(d):
+            @pl.when(place(d) < n - 1)
+            def _():
+                for p in range(1, n + 1):
+                    along(d, p, c, rs.at[0, 0], rs.at[0, 0]).wait_send()
+
+        each(2, line)
+        x_grad(c).wait_send()
+        x_out(c).wait_send()
+        for level in range(levels):
+            swap(level, c).wait_send()
+        store_m(c).wait()
+        store_y(c).wait()
+        store_n(c).wait()
+
+    each(chunks, ends)
+
+    def unit_ends(u):
+        x_context(u).wait_send()
+        x_back(u).wait_send()
+
+    each(n, unit_ends)
+
+    def head_ends(h):
+        for a in range(3):
+            store_head(a, h).wait()
+
+    each(heads, head_ends)
+
+
+def line_shape(count, levels, tokens, features, rows, columns):
+    n = count // 2
+    heads = features // HEAD_SIZE
+    wide = 4 * LANES
+    fits = (
+        count % 2 == 0
+        and n == 4
+        and levels >= 1
+        and tokens % LANES == 0
+        and rows % 16 == 0
+        and heads % n == 0
+        and 2 * rows * n == features
+        and columns % wide == 0
+        and columns // wide >= 5
+    )
+    return (n, wide) if fits else None
+
+
+def on_line(
+    n, wide, query, key, value, residual, out_grad, doc_ids, weight, momentum, step_index
+):
+    tokens, features = query.shape
+    rows, columns = weight.shape
+    chunks = columns // wide
+    heads = features // HEAD_SIZE
+    levels = lax.axis_size("rep").bit_length() - 1
+    any_space = pl.BlockSpec(memory_space=pl.ANY)
+    low, full = jnp.bfloat16, jnp.float32
+    dma = pltpu.SemaphoreType.DMA
+    like = lambda a: jax.ShapeDtypeStruct(a.shape, a.dtype)
+    return pl.pallas_call(
+        functools.partial(line_kernel, n, levels),
+        in_specs=[any_space] * 7
+        + [pl.BlockSpec(memory_space=pltpu.VMEM), pl.BlockSpec(memory_space=pltpu.SMEM)],
+        out_specs=[any_space] * 6,
+        out_shape=[like(a) for a in (residual, query, key, value, weight, momentum)],
+        scratch_shapes=[
+            pltpu.VMEM((n, chunks, rows, wide), low),
+            pltpu.VMEM((chunks, tokens, wide), low),
+            pltpu.VMEM((chunks, tokens, wide), low),
+            pltpu.VMEM((heads, tokens, HEAD_SIZE), low),
+            pltpu.VMEM((heads, tokens, HEAD_SIZE), low),
+            pltpu.VMEM((heads, tokens, HEAD_SIZE), low),
+            pltpu.VMEM((features, tokens), low),
+            pltpu.VMEM((n, rows, tokens), low),
+            pltpu.VMEM((features, tokens), low),
+            pltpu.VMEM((n, rows, tokens), low),
+            pltpu.VMEM((2, rows, tokens), full),
+            pltpu.VMEM((2, chunks, tokens, wide), full),
+            pltpu.VMEM((chunks, tokens, wide), low),
+            pltpu.VMEM((chunks, tokens, wide), low),
+            pltpu.VMEM((n + 1, chunks, rows, wide), low),
+            pltpu.VMEM((chunks, rows, wide), full),
+            pltpu.VMEM((chunks, rows, wide), low),
+            pltpu.VMEM((levels, chunks, rows, wide), low),
+            pltpu.VMEM((chunks, tokens, wide), low),
+            pltpu.VMEM((tokens, tokens), full),
+            dma((3, heads)),
+            dma((chunks,)),
+            dma((chunks,)),
+            dma((chunks,)),
+            dma((chunks,)),
+            dma((chunks,)),
+            dma((chunks,)),
+            dma((chunks,)),
+            dma((n,)),
+            dma((n,)),
+            dma((n,)),
+            dma((n,)),
+            dma((chunks,)),
+            dma((chunks,)),
+            dma((2, n, chunks)),
+            dma((2, n, chunks)),
+            dma((levels, chunks)),
+            dma((levels, chunks)),
+        ],
+        compiler_params=pltpu.CompilerParams(
+            collective_id=0, has_side_effects=True, vmem_limit_bytes=67043328
+        ),
+    )(
+        query,
+        key,
+        value,
+        residual,
+        out_grad,
+        weight,
+        momentum,
+        doc_ids,
+        step_index,
+    )
+
+
 def on_device(
     query_rows,
     key_rows,
@@ -103,6 +687,20 @@
     step_index,
 ):
     count = lax.axis_size("fsdp")
+    shape = line_shape(
+        count,
+        lax.axis_size("rep").bit_length() - 1,
+        query_rows.shape[1],
+        query_rows.shape[2],
+        out_weight.shape[1],
+        out_weight.shape[2],
+    )
+    if shape is not None:
+        arrays = (query_rows, key_rows, value_rows, residual_in, out_grad)
+        results = on_line(
+            *shape, *[a[0] for a in arrays], doc_ids, out_weight[0], momentum[0], step_index
+        )
+        return tuple(r[None] for r in results)
     side = lax.axis_index("fsdp") % 2
     groups = [[i for i in range(count) if i % 2 == s] for s in range(2)]
     pair = [(i, i ^ 1) for i in range(count)]

time: 266 us -> 175 us (0.66)
  waiting for transfers between devices: 156 us -> 0 us
  Pallas kernels: 37 us -> 159 us
  matrix products: 28.6 us -> 0 us
  between operations: 14.8 us -> 1.3 us
  other arithmetic: 12.7 us -> 0 us
  starting transfers between devices: 5.3 us -> 0 us
  local copies, waits for them, and re-layouts: 11.1 us -> 14 us
    pallas_call x2 -> x1, Pallas kernels: 37 us -> 159 us  [on_line(): pl.pallas_call(functools.partial(line_kernel, n, levels), in_specs=[any_s...]
    ppermute x5 -> x0, waiting for transfers between devices: 68.4 us -> none  [the longest x1 39.7 us: on_device(): pair_context = lax.ppermute(jnp.where(first, high, low), 'fsdp', pair)]
    all_gather x1 -> x0, waiting for transfers between devices: 48.7 us -> none  [on_device(): lax.all_gather(weight_shard, 'fsdp', axis=0, tiled=True, axis_index_group...]
    reduce_scatter x1 -> x0, waiting for transfers between devices: 38.7 us -> none  [on_device(): lax.psum_scatter(weight_term, 'fsdp', scatter_dimension=0, tiled=True, ax...]
    dot_general x6 -> x0, matrix products: 28.6 us -> none  [the longest x2 11 us: outer(): lax.dot_general(left, right, (((0,), (0,)), ((), ())), preferred_element_...]
    unnamed x10 -> x16, local copies, waits for them, and re-layouts: 1.37 us -> 14 us
    broadcast_in_dim x3 -> x0, other arithmetic: 12.5 us -> none  [the longest x1 4.89 us: on_device(): new_momentum[None]]
    concatenate x3 -> x0, local copies, waits for them, and re-layouts: 5.36 us -> none  [the longest x1 3.98 us: on_device(): context_grad = jnp.concatenate(pieces, axis=1)]
  transfers between devices with their start and end apart: 7 -> 0, of which waited for: 6 -> 0; matrix products, arithmetic and copies ran while one was open for 16% -> 0% of each run, Pallas kernels for 14% -> 0%
where the time goes in v1:
time: 175 us; the launch traced here: 174 us
  Pallas kernels  159 us (91%)
  local copies, waits for them, and re-layouts  14 us (8%)
    pallas_call x1, Pallas kernels, on_line(): pl.pallas_call(functools.partial(line_kernel, n, levels), in_specs=[any_s...  159 us
    unnamed x16, local copies, waits for them, and re-layouts  14 us

profile of v1, /device:TPU:0, one launch (start us, length us, event | category | flops | bytes accessed | tf_op | source)
XLA Modules:
  0.0 174.5 jit_solution(2535570901417896870)
XLA Ops:
  1.3 159.2 %shard_map.136 = (bf16[384,2560]{1,0:T(8,128)(2,1)}, bf16[384,2560]{1,0:T(8,128)(2,1)}, bf16[384,2560]{1,0:T(8,128)(2,1)}, bf16[384,2560]{1,0:T(8,128)(2,1)}, bf...) custom-call(bf16[384,2560]{1,0:T(8,128)(2,1)} %bitcast.15, bf16[384,2560]{1,0:T(8,128)(2,1)} %bitcast.16, ...), custom_call_target="tpu_custom_call" | custom-call | tf_op jit(solution)/shard_map/pallas_call | solution.py:616
  160.5 0.0 copy-start.3
  160.5 3.1 %copy.22 = bf16[1,384,2560]{2,1,0:T(8,128)(2,1)} copy(bf16[1,384,2560]{2,1,0:T(8,128)(2,1)} %bitcast.23) | data formatting | bytes 3932160
  163.6 0.0 copy-done.3
  163.6 0.0 copy-start.2
  163.6 1.3 copy.23
  164.9 1.0 copy-done.2
  165.8 0.0 copy-start.1
  165.8 1.3 copy.24
  167.1 1.0 copy-done.1
  168.1 0.0 copy-start.4
  168.1 1.3 copy.25
  169.4 0.9 copy-done.4
  170.2 0.0 copy-start
  170.2 1.2 copy.26
  171.4 1.4 copy-done
  172.8 1.7 copy.27
Async XLA Ops:
  160.5 3.1 %copy-start.3 = (bf16[384,2560]{1,0:T(8,128)(2,1)S(1)}, bf16[384,2560]{1,0:T(8,128)(2,1)}, u32[]{:S(2)}) copy-start(bf16[384,2560]{1,0:T(8,128)(2,1)} %get-tuple-element.13) | copy-start | bytes 5898244
  163.6 2.3 %copy-start.2 = (bf16[384,2560]{1,0:T(8,128)(2,1)S(1)}, bf16[384,2560]{1,0:T(8,128)(2,1)}, u32[]{:S(2)}) copy-start(bf16[384,2560]{1,0:T(8,128)(2,1)} %get-tuple-element.14) | copy-start | bytes 5898244
  165.8 2.3 %copy-start.1 = (bf16[384,2560]{1,0:T(8,128)(2,1)S(1)}, bf16[384,2560]{1,0:T(8,128)(2,1)}, u32[]{:S(2)}) copy-start(bf16[384,2560]{1,0:T(8,128)(2,1)} %get-tuple-element.15) | copy-start | bytes 5898244
  168.1 2.1 %copy-start.4 = (bf16[320,2560]{1,0:T(8,128)(2,1)S(1)}, bf16[320,2560]{1,0:T(8,128)(2,1)}, u32[]{:S(2)}) copy-start(bf16[320,2560]{1,0:T(8,128)(2,1)} %get-tuple-element.16) | copy-start | bytes 4915204
  170.2 2.5 %copy-start = (f32[320,2560]{1,0:T(8,128)S(1)}, f32[320,2560]{1,0:T(8,128)}, u32[]{:S(2)}) copy-start(f32[320,2560]{1,0:T(8,128)} %get-tuple-element.17) | copy-start | bytes 9830404

commit v2 on v1

--- a/solution.py
+++ b/solution.py
@@ -113,18 +113,15 @@
     mom_hbm,
     doc_ref,
     step_ref,
-    out_hbm,
-    dq_hbm,
-    dk_hbm,
-    dv_hbm,
-    nw_hbm,
-    nm_hbm,
+    rb,
+    qb,
+    kb,
+    vb,
+    nb,
+    mb,
     wbuf,
     gown,
     gpair,
-    qb,
-    kb,
-    vb,
     ctx,
     ctxp,
     cg,
@@ -134,17 +131,14 @@
     osend,
     ogot,
     rs,
-    mb,
     st,
     pr,
-    rb,
     bias,
     hs,
     ws,
     gs,
     ms,
     ys,
-    ns,
     xg_s,
     xg_r,
     xc_s,
@@ -190,11 +184,6 @@
         dst = (qb, kb, vb)[i]
         return pltpu.make_async_copy(src.at[:, lanes(h, size)], dst.at[h], hs.at[i, h])
 
-    def store_head(i, h):
-        src = (qb, kb, vb)[i]
-        dst = (dq_hbm, dk_hbm, dv_hbm)[i]
-        return pltpu.make_async_copy(src.at[h], dst.at[:, lanes(h, size)], hs.at[i, h])
-
     def load_w(c):
         return pltpu.make_async_copy(w_hbm.at[:, lanes(c, wide)], wbuf.at[z, c], ws.at[c])
 
@@ -204,17 +193,8 @@
     def load_m(c):
         return pltpu.make_async_copy(mom_hbm.at[:, lanes(c, wide)], mb.at[c], ms.at[c])
 
-    def store_m(c):
-        return pltpu.make_async_copy(mb.at[c], nm_hbm.at[:, lanes(c, wide)], ms.at[c])
-
     def load_y(c):
         return pltpu.make_async_copy(res_hbm.at[:, lanes(c, wide)], rb.at[c], ys.at[c])
-
-    def store_y(c):
-        return pltpu.make_async_copy(rb.at[c], out_hbm.at[:, lanes(c, wide)], ys.at[c])
-
-    def store_n(c):
-        return pltpu.make_async_copy(pr.at[0, c], nw_hbm.at[:, lanes(c, wide)], ns.at[c])
 
     def to_pair(src, dst, send, recv):
         return pltpu.make_async_remote_copy(
@@ -396,10 +376,7 @@
         x_back(u).wait_recv()
 
         def one(hh):
-            h = u * per + hh
-            backward_head(h)
-            for a in range(3):
-                store_head(a, h).start()
+            backward_head(u * per + hh)
 
         each(per, one)
 
@@ -432,13 +409,11 @@
         mb[c] = moment
         stepped = wbuf[z, c].astype(jnp.float32) - learning_rate * moment
         st[c] = stepped.astype(jnp.bfloat16)
-        store_m(c).start()
         for level in range(levels):
             swap(level, c).start()
         x_out(c).wait_recv()
         total_out = rb[c].astype(jnp.float32) + oacc[0, c] + ogot[c].astype(jnp.float32)
         rb[c] = total_out.astype(jnp.bfloat16)
-        store_y(c).start()
 
     def average(c):
         for level in range(levels):
@@ -448,8 +423,7 @@
         for level in range(levels - 1):
             other = jnp.where(level_now == level, pr[level, c].astype(jnp.float32), other)
         mean = (st[c].astype(jnp.float32) + other) * 0.5
-        pr[0, c] = mean.astype(jnp.bfloat16)
-        store_n(c).start()
+        nb[c] = mean.astype(jnp.bfloat16)
 
     def step(t):
         p = 2 + lax.div(t, chunks)
@@ -564,9 +538,6 @@
         x_out(c).wait_send()
         for level in range(levels):
             swap(level, c).wait_send()
-        store_m(c).wait()
-        store_y(c).wait()
-        store_n(c).wait()
 
     each(chunks, ends)
 
@@ -576,11 +547,47 @@
 
     each(n, unit_ends)
 
-    def head_ends(h):
-        for a in range(3):
-            store_head(a, h).wait()
-
-    each(heads, head_ends)
+
+def write_kernel(
+    rb, qb, kb, vb, nb, mb, out_hbm, dq_hbm, dk_hbm, dv_hbm, nw_hbm, nm_hbm, hs, cs
+):
+    heads, _, size = qb.shape
+    chunks, _, wide = rb.shape
+
+    def head(h):
+        lanes = pl.ds(pl.multiple_of(h * size, size), size)
+        return [
+            pltpu.make_async_copy(src.at[h], dst.at[:, lanes], hs.at[i, h])
+            for i, (src, dst) in enumerate(((qb, dq_hbm), (kb, dk_hbm), (vb, dv_hbm)))
+        ]
+
+    def chunk(c):
+        lanes = pl.ds(pl.multiple_of(c * wide, wide), wide)
+        return [
+            pltpu.make_async_copy(src.at[c], dst.at[:, lanes], cs.at[i, c])
+            for i, (src, dst) in enumerate(((rb, out_hbm), (nb, nw_hbm), (mb, nm_hbm)))
+        ]
+
+    def start(count, copies):
+        def one(i, carry):
+            for copy in copies(i):
+                copy.start()
+            return carry
+
+        lax.fori_loop(0, count, one, 0)
+
+    def wait(count, copies):
+        def one(i, carry):
+            for copy in copies(i):
+                copy.wait()
+            return carry
+
+        lax.fori_loop(0, count, one, 0)
+
+    start(chunks, chunk)
+    start(heads, head)
+    wait(chunks, chunk)
+    wait(heads, head)
 
 
 def line_shape(count, levels, tokens, features, rows, columns):
@@ -610,22 +617,27 @@
     heads = features // HEAD_SIZE
     levels = lax.axis_size("rep").bit_length() - 1
     any_space = pl.BlockSpec(memory_space=pl.ANY)
+    in_vmem = pl.BlockSpec(memory_space=pltpu.VMEM)
     low, full = jnp.bfloat16, jnp.float32
     dma = pltpu.SemaphoreType.DMA
     like = lambda a: jax.ShapeDtypeStruct(a.shape, a.dtype)
-    return pl.pallas_call(
+    by_head = pltpu.VMEM((heads, tokens, HEAD_SIZE), low)
+    held = pl.pallas_call(
         functools.partial(line_kernel, n, levels),
-        in_specs=[any_space] * 7
-        + [pl.BlockSpec(memory_space=pltpu.VMEM), pl.BlockSpec(memory_space=pltpu.SMEM)],
-        out_specs=[any_space] * 6,
-        out_shape=[like(a) for a in (residual, query, key, value, weight, momentum)],
+        in_specs=[any_space] * 7 + [in_vmem, pl.BlockSpec(memory_space=pltpu.SMEM)],
+        out_specs=[in_vmem] * 6,
+        out_shape=[
+            pltpu.VMEM((chunks, tokens, wide), low),
+            by_head,
+            by_head,
+            by_head,
+            pltpu.VMEM((chunks, rows, wide), low),
+            pltpu.VMEM((chunks, rows, wide), full),
+        ],
         scratch_shapes=[
             pltpu.VMEM((n, chunks, rows, wide), low),
             pltpu.VMEM((chunks, tokens, wide), low),
             pltpu.VMEM((chunks, tokens, wide), low),
-            pltpu.VMEM((heads, tokens, HEAD_SIZE), low),
-            pltpu.VMEM((heads, tokens, HEAD_SIZE), low),
-            pltpu.VMEM((heads, tokens, HEAD_SIZE), low),
             pltpu.VMEM((features, tokens), low),
             pltpu.VMEM((n, rows, tokens), low),
             pltpu.VMEM((features, tokens), low),
@@ -635,13 +647,10 @@
             pltpu.VMEM((chunks, tokens, wide), low),
             pltpu.VMEM((chunks, tokens, wide), low),
             pltpu.VMEM((n + 1, chunks, rows, wide), low),
-            pltpu.VMEM((chunks, rows, wide), full),
             pltpu.VMEM((chunks, rows, wide), low),
             pltpu.VMEM((levels, chunks, rows, wide), low),
-            pltpu.VMEM((chunks, tokens, wide), low),
             pltpu.VMEM((tokens, tokens), full),
             dma((3, heads)),
-            dma((chunks,)),
             dma((chunks,)),
             dma((chunks,)),
             dma((chunks,)),
@@ -660,7 +669,7 @@
             dma((levels, chunks)),
         ],
         compiler_params=pltpu.CompilerParams(
-            collective_id=0, has_side_effects=True, vmem_limit_bytes=67043328
+            collective_id=0, has_side_effects=True, vmem_limit_bytes=50 << 20
         ),
     )(
         query,
@@ -673,6 +682,14 @@
         doc_ids,
         step_index,
     )
+    return pl.pallas_call(
+        write_kernel,
+        in_specs=[any_space] * 6,
+        out_specs=[any_space] * 6,
+        out_shape=[like(a) for a in (residual, query, key, value, weight, momentum)],
+        scratch_shapes=[dma((3, heads)), dma((3, chunks))],
+        compiler_params=pltpu.CompilerParams(vmem_limit_bytes=1 << 20),
+    )(*held)
 
 
 def on_device(

time: 175 us -> 165 us (0.943)
  local copies, waits for them, and re-layouts: 14 us -> 0 us
  Pallas kernels: 159 us -> 164 us
    unnamed x16 -> x0, local copies, waits for them, and re-layouts: 14 us -> none
    pallas_call x0 -> x1, Pallas kernels: none -> 5.25 us  [on_line(): pl.pallas_call(write_kernel, in_specs=[any_space] * 6, out_specs=[any_spa...]
where the time goes in v2:
time: 165 us
  Pallas kernels  164 us (99%)
    pallas_call x1, Pallas kernels, on_line(): pl.pallas_call(functools.partial(line_kernel, n, levels), in_specs=[any_s...  158 us
    pallas_call x1, Pallas kernels, on_line(): pl.pallas_call(write_kernel, in_specs=[any_space] * 6, out_specs=[any_spa...  5.25 us

profile of v2, /device:TPU:0, one launch (start us, length us, event | category | flops | bytes accessed | tf_op | source)
XLA Modules:
  0.0 165.0 jit_solution(7381865539079397008)
XLA Ops:
  1.3 158.5 %shard_map.136 = (bf16[5,384,512]{2,1,0:T(8,128)(2,1)S(1)}, bf16[20,384,128]{2,1,0:T(8,128)(2,1)S(1)}, bf16[20,384,128]{2,1,0:T(8,128)(2,1)S(1)}, bf16[20,384,12...) custom-call(bf16[384,2560]{1,0:T(8,128)(2,1)} %bitcast.14, ...), custom_call_target="tpu_custom_call" | custom-call | tf_op jit(solution)/shard_map/pallas_call | solution.py:625
  159.8 5.3 %shard_map.137 = (bf16[384,2560]{1,0:T(8,128)(2,1)}, bf16[384,2560]{1,0:T(8,128)(2,1)}, bf16[384,2560]{1,0:T(8,128)(2,1)}, bf16[384,2560]{1,0:T(8,128)(2,1)}, bf...) custom-call(bf16[5,384,512]{2,1,0:T(8,128)(2,1)S(1)} %get-tuple-element.18.rb, ...), custom_call_target="tpu_custom_call" | custom-call | tf_op jit(solution)/shard_map/pallas_call | solution.py:685

commit v3 on v2

--- a/solution.py
+++ b/solution.py
@@ -93,12 +93,24 @@
 
 MESH = pl.DeviceIdType.MESH
 LANES = 128
+COARSE, FINE = 2, 2
 
 
 def dot(a, b, ca, cb):
     return lax.dot_general(
         a, b, (((ca,), (cb,)), ((), ())), preferred_element_type=jnp.float32
     )
+
+
+def step_order(n, chunks):
+    order = [(p, c) for p in range(2, n) for c in range(chunks)]
+    head, ahead = order[: chunks * (n - 3) + 3], order[chunks * (n - 3) + 3 :]
+    tail = [(n, 0), ahead[0], (n, 1)] + ahead[1:] + [(n, 2)]
+    tail += [(n + 1, 0)]
+    for c in range(3, chunks):
+        tail += [(n, c), (n + 1, c - 2)]
+    tail += [(n + 1, c) for c in range(chunks - 2, chunks)]
+    return head + tail
 
 
 def line_kernel(
@@ -111,8 +123,8 @@
     g_hbm,
     w_hbm,
     mom_hbm,
-    doc_ref,
-    step_ref,
+    doc_hbm,
+    step_hbm,
     rb,
     qb,
     kb,
@@ -134,6 +146,10 @@
     st,
     pr,
     bias,
+    own,
+    doc_ref,
+    step_ref,
+    ds,
     hs,
     ws,
     gs,
@@ -149,11 +165,14 @@
     xo_r,
     zs,
     zr,
+    fs,
+    fr,
     ps,
     pr_r,
 ):
     units, chunks, rows, wide = wbuf.shape
-    heads, tokens, size = qb.shape
+    size = HEAD_SIZE
+    tokens, heads = qb.shape[0], qb.shape[1] // size
     per = heads // n
     scale = HEAD_SIZE ** (-0.5)
     me = lax.axis_index("fsdp")
@@ -176,13 +195,25 @@
     def pair_rows(u):
         return pl.ds(pl.multiple_of((2 * u + 1 - x) * rows, 16), rows)
 
+    def each_part(c, body):
+        @pl.when(c < chunks - 1)
+        def _():
+            each(COARSE, lambda s: body(c, s, rows // COARSE))
+
+        @pl.when(c == chunks - 1)
+        def _():
+            each(FINE, lambda s: body(c, s, rows // FINE))
+
+    def cut_rows(s, part):
+        return pl.ds(pl.multiple_of(s * part, 16), part)
+
     def head_rows(h):
         return pl.ds(pl.multiple_of(h * size, size), size)
 
     def load_head(i, h):
         src = (q_hbm, k_hbm, v_hbm)[i]
         dst = (qb, kb, vb)[i]
-        return pltpu.make_async_copy(src.at[:, lanes(h, size)], dst.at[h], hs.at[i, h])
+        return pltpu.make_async_copy(src.at[:, lanes(h, size)], dst.at[:, lanes(h, size)], hs.at[i, h])
 
     def load_w(c):
         return pltpu.make_async_copy(w_hbm.at[:, lanes(c, wide)], wbuf.at[z, c], ws.at[c])
@@ -191,10 +222,10 @@
         return pltpu.make_async_copy(g_hbm.at[:, lanes(c, wide)], gown.at[c], gs.at[c])
 
     def load_m(c):
-        return pltpu.make_async_copy(mom_hbm.at[:, lanes(c, wide)], mb.at[c], ms.at[c])
+        return pltpu.make_async_copy(mom_hbm.at[:, lanes(c, wide)], mb.at[:, lanes(c, wide)], ms.at[c])
 
     def load_y(c):
-        return pltpu.make_async_copy(res_hbm.at[:, lanes(c, wide)], rb.at[c], ys.at[c])
+        return pltpu.make_async_copy(res_hbm.at[:, lanes(c, wide)], rb.at[:, lanes(c, wide)], ys.at[c])
 
     def to_pair(src, dst, send, recv):
         return pltpu.make_async_remote_copy(
@@ -228,15 +259,25 @@
             device_id_type=MESH,
         )
 
+    def along_last(d, c, s, part, src, dst):
+        return pltpu.make_async_remote_copy(
+            src_ref=src.at[cut_rows(s, part), :],
+            dst_ref=dst.at[cut_rows(s, part), :],
+            send_sem=fs.at[d, c, s],
+            recv_sem=fr.at[d, c, s],
+            device_id={"fsdp": me + 2 - 4 * d},
+            device_id_type=MESH,
+        )
+
     def place(d):
         return z + d * (n - 1 - 2 * z)
 
-    def swap(level, c):
+    def swap(level, c, s, part):
         return pltpu.make_async_remote_copy(
-            src_ref=st.at[c],
-            dst_ref=pr.at[level, c],
-            send_sem=ps.at[level, c],
-            recv_sem=pr_r.at[level, c],
+            src_ref=st.at[c, cut_rows(s, part), :],
+            dst_ref=pr.at[level, c, cut_rows(s, part), :],
+            send_sem=ps.at[level, c, s],
+            recv_sem=pr_r.at[level, c, s],
             device_id={"rep": partner(level)},
             device_id_type=MESH,
         )
@@ -259,8 +300,6 @@
                 load_head(a, u * per + hh).start()
 
         each(per, one)
-
-    start_loads(0)
 
     barrier = pltpu.get_barrier_semaphore()
     pl.semaphore_signal(barrier, inc=1, device_id={"fsdp": pair}, device_id_type=MESH)
@@ -289,7 +328,11 @@
 
     each(chunks, first_sends)
     x_grad(0).start()
-    each(n - 1, lambda i: start_loads(i + 1))
+    load_doc = pltpu.make_async_copy(doc_hbm, doc_ref, ds.at[0])
+    load_step = pltpu.make_async_copy(step_hbm, step_ref, ds.at[1])
+    load_doc.start()
+    load_step.start()
+    each(n, start_loads)
 
     def other_loads(c):
         load_g(c).start()
@@ -299,6 +342,8 @@
 
     each(chunks, other_loads)
 
+    load_doc.wait()
+    load_step.wait()
     row_ids = jnp.broadcast_to(doc_ref[...], (tokens, tokens))
     column_ids = jnp.transpose(row_ids)
     r = lax.broadcasted_iota(jnp.int32, (tokens, tokens), 0)
@@ -315,7 +360,8 @@
         return exponents * (1.0 / jnp.sum(exponents, axis=-1, keepdims=True))
 
     def forward_head(h):
-        q, k, v = qb[h], kb[h], vb[h]
+        cut_h = lanes(h, size)
+        q, k, v = qb[:, cut_h], kb[:, cut_h], vb[:, cut_h]
         parts = []
         for i in range(blocks):
             probs = probabilities_of(q, k, i).astype(jnp.bfloat16)
@@ -350,7 +396,8 @@
     each(chunks, wait_loads)
 
     def backward_head(h):
-        q, k, v = qb[h], kb[h], vb[h]
+        cut_h = lanes(h, size)
+        q, k, v = qb[:, cut_h], kb[:, cut_h], vb[:, cut_h]
         grad = jnp.transpose(cg[head_rows(h), :].astype(jnp.float32)).astype(jnp.bfloat16)
         low, score_grads, parts = [], [], []
         for i in range(blocks):
@@ -364,72 +411,156 @@
             parts.append(dot(score_grad, k[:seen], 1, 0))
         for i in range(blocks):
             cut = slice(i * LANES, (i + 1) * LANES)
-            qb[h, cut, :] = parts[i].astype(jnp.bfloat16)
+            qb[cut, cut_h] = parts[i].astype(jnp.bfloat16)
         for j in range(blocks):
             cut = slice(j * LANES, (j + 1) * LANES)
             scores_j = jnp.concatenate([b[:, cut] for b in score_grads[j:]], axis=0)
             probs_j = jnp.concatenate([b[:, cut] for b in low[j:]], axis=0)
-            kb[h, cut, :] = dot(scores_j, q[j * LANES :], 0, 0).astype(jnp.bfloat16)
-            vb[h, cut, :] = dot(probs_j, grad[j * LANES :], 0, 0).astype(jnp.bfloat16)
-
-    def backward_unit(u):
-        x_back(u).wait_recv()
-
-        def one(hh):
+            kb[cut, cut_h] = dot(scores_j, q[j * LANES :], 0, 0).astype(jnp.bfloat16)
+            vb[cut, cut_h] = dot(probs_j, grad[j * LANES :], 0, 0).astype(jnp.bfloat16)
+
+    def backward_heads(u, low, high):
+        @pl.when(low == 0)
+        def _():
+            x_back(u).wait_recv()
+
+        def one(hh, carry):
             backward_head(u * per + hh)
-
-        each(per, one)
+            return carry
+
+        lax.fori_loop(low, high, one, 0)
 
     def weight_part(u, c):
         return dot(ctx[own_rows(u), :], gown[c], 1, 0) + dot(ctxp[u], gpair[c], 1, 0)
 
-    def unit_chunk(u, c):
+    def unit_chunk(i, u, c):
         weight = wbuf[u, c]
         for side in range(2):
             left = ctx[own_rows(u), :] if side == 0 else ctxp[u]
             grad = gown[c] if side == 0 else gpair[c]
             before = jnp.where(u == z, 0.0, oacc[side, c])
             oacc[side, c] = before + dot(left, weight, 0, 0)
-            before = jnp.where(c == 0, 0.0, acc[side])
-            acc[side] = before + dot(weight, grad, 1, 1)
+            before = jnp.where(c == 0, 0.0, acc[i, side])
+            acc[i, side] = before + dot(weight, grad, 1, 1)
 
         @pl.when(c == chunks - 1)
         def _():
-            cgs[u] = acc[1].astype(jnp.bfloat16)
-            cg[own_rows(u), :] = acc[0].astype(jnp.bfloat16)
+            cgs[u] = acc[i, 1].astype(jnp.bfloat16)
+            cg[own_rows(u), :] = acc[i, 0].astype(jnp.bfloat16)
             x_back(u).start()
 
     far = jnp.where(2 * z < n, z + 2, z - 2)
 
+    def finish_part(c, s, part):
+        def arrived(d):
+            @pl.when(place(d) > 0)
+            def _():
+                along_last(d, c, s, part, rs.at[0, 0], rs.at[0, 0]).wait_recv()
+
+        each(2, arrived)
+        cut, across = cut_rows(s, part), lanes(c, wide)
+        total = own[cut, :]
+        total = total + jnp.where(z > 0, rs[z, c, cut, :].astype(jnp.float32), 0.0)
+        total = total + jnp.where(z < n - 1, rs[n, c, cut, :].astype(jnp.float32), 0.0)
+        moment = momentum_decay * mb[cut, across] + total
+        mb[cut, across] = moment
+        stepped = wbuf[z, c, cut, :].astype(jnp.float32) - learning_rate * moment
+        st[c, cut, :] = stepped.astype(jnp.bfloat16)
+        for level in range(levels):
+            swap(level, c, s, part).start()
+        a, b = min(2, per), min(3, per)
+        u, low, high = pick(
+            [
+                (at_end & (c == 0) & (s == 1), (far, 0, per)),
+                (at_end & (c == chunks - 3) & (s == 1), (last, 0, a)),
+                (at_end & (c == chunks - 2) & (s == 0), (last, a, b)),
+                (at_end & (c == chunks - 2) & (s == 1), (last, b, min(4, per))),
+                (at_end & (c == chunks - 1) & (s == 0), (last, min(4, per), per)),
+                (~at_end & (c == 0) & (s == 1), (z + 1, 0, per)),
+                (~at_end & (c == 1) & (s == 1), (far, 0, per)),
+            ]
+        )
+
+        @pl.when(u >= 0)
+        def _():
+            backward_heads(u, low, high)
+
+    def average(c, s, part):
+        cut = cut_rows(s, part)
+        for level in range(levels):
+            swap(level, c, s, part).wait()
+        level_now = jnp.full((part, wide), lax.rem(step_ref[0], levels), jnp.int32)
+        other = pr[levels - 1, c, cut, :].astype(jnp.float32)
+        for level in range(levels - 1):
+            before = pr[level, c, cut, :].astype(jnp.float32)
+            other = jnp.where(level_now == level, before, other)
+        mean = (st[c, cut, :].astype(jnp.float32) + other) * 0.5
+        nb[cut, lanes(c, wide)] = mean.astype(jnp.bfloat16)
+
+    def pick(cases):
+        values = (-1, 0, 0)
+        for condition, choice in cases:
+            values = tuple(jnp.where(condition, a, b) for a, b in zip(choice, values))
+        return values
+
+    last = n - 1 - z
+    first_side = jnp.where(z > 0, z - 1, z + 1)
+
+    def early_sent(c):
+        def line(d):
+            @pl.when(place(d) < n - 1)
+            def _():
+                for p in range(1, n):
+                    along(d, p, c, rs.at[0, 0], rs.at[0, 0]).wait_send()
+
+        each(2, line)
+        x_grad(c).wait_send()
+
+    def unit_sent(u):
+        x_context(u).wait_send()
+        x_back(u).wait_send()
+
+    def last_sent(c):
+        def line(d):
+            @pl.when(place(d) < n - 1)
+            def _():
+                each_part(
+                    c,
+                    lambda c, s, part: along_last(
+                        d, c, s, part, rs.at[0, 0], rs.at[0, 0]
+                    ).wait_send(),
+                )
+
+        each(2, line)
+        x_out(c).wait_send()
+
     def finish(c):
-        total = weight_part(z, c)
-        total = total + jnp.where(z > 0, rs[z, c].astype(jnp.float32), 0.0)
-        total = total + jnp.where(z < n - 1, rs[n, c].astype(jnp.float32), 0.0)
-        moment = momentum_decay * mb[c] + total
-        mb[c] = moment
-        stepped = wbuf[z, c].astype(jnp.float32) - learning_rate * moment
-        st[c] = stepped.astype(jnp.bfloat16)
-        for level in range(levels):
-            swap(level, c).start()
+        own[...] = weight_part(z, c)
+        each_part(c, finish_part)
         x_out(c).wait_recv()
-        total_out = rb[c].astype(jnp.float32) + oacc[0, c] + ogot[c].astype(jnp.float32)
-        rb[c] = total_out.astype(jnp.bfloat16)
-
-    def average(c):
-        for level in range(levels):
-            swap(level, c).wait_recv()
-        level_now = jnp.full((rows, wide), lax.rem(step_ref[0], levels), jnp.int32)
-        other = pr[levels - 1, c].astype(jnp.float32)
-        for level in range(levels - 1):
-            other = jnp.where(level_now == level, pr[level, c].astype(jnp.float32), other)
-        mean = (st[c].astype(jnp.float32) + other) * 0.5
-        nb[c] = mean.astype(jnp.bfloat16)
+        across = lanes(c, wide)
+        total_out = rb[:, across].astype(jnp.float32) + oacc[0, c]
+        rb[:, across] = (total_out + ogot[c].astype(jnp.float32)).astype(jnp.bfloat16)
+
+        @pl.when(c > 0)
+        def _():
+            each_part(c - 1, average)
+            last_sent(c - 1)
+
+        @pl.when(c == chunks - 2)
+        def _():
+            each(chunks, early_sent)
+
+    order = step_order(n, chunks)
 
     def step(t):
-        p = 2 + lax.div(t, chunks)
-        c = lax.rem(t, chunks)
-
-        @pl.when(p <= n + 1)
+        code = 0
+        for i, (p, c) in enumerate(order):
+            code = jnp.where(t == i, p * chunks + c, code)
+        p = lax.div(code, chunks)
+        c = lax.rem(code, chunks)
+
+        @pl.when(p <= n)
         def _():
             def arrived(d):
                 @pl.when(place(d) > 0)
@@ -438,8 +569,6 @@
 
             each(2, arrived)
 
-        @pl.when(p <= n)
-        def _():
             def forward(d):
                 zz = place(d)
 
@@ -472,36 +601,41 @@
                     b = b + d * (n - 1 - 2 * b)
                     before = jnp.where(zz > 0, rs[b, c].astype(jnp.float32), 0.0)
                     rs[b, c] = (before + weight_part(b, c)).astype(jnp.bfloat16)
-                    slot = jnp.where((p == n) & (d == 1), n, b)
-                    along(d, p, c, rs.at[b, c], rs.at[slot, c]).start()
+
+                    @pl.when(p < n)
+                    def _():
+                        along(d, p, c, rs.at[b, c], rs.at[b, c]).start()
+
+                    @pl.when(p == n)
+                    def _():
+                        slot = jnp.where(d == 1, n, b)
+                        each_part(
+                            c,
+                            lambda c, s, part: along_last(
+                                d, c, s, part, rs.at[b, c], rs.at[slot, c]
+                            ).start(),
+                        )
 
             each(2, reduce)
 
-        @pl.when(p == n + 1)
-        def _():
-            finish(c)
-
-        @pl.when(t >= (n - 1) * chunks + 1)
-        def _():
-            average(t - ((n - 1) * chunks + 1))
-
         @pl.when((p == 3) | (p == 4))
         def _():
             def unit(i):
-                whole = jnp.where(
-                    p == 3,
-                    jnp.where(c == 0, z, jnp.where(c == 1, z - 1, jnp.where(c == 2, z + 1, -1))),
-                    jnp.where(c == 0, far, -1),
+                u, low, high = pick(
+                    [
+                        ((i == 0) & (p == 3) & (c == 0), (z, 0, chunks)),
+                        ((i == 0) & (p == 3) & (c == 1), (z - 1, 0, chunks)),
+                        ((i == 0) & (p == 3) & (c == 2) & (z < n - 1), (z + 1, 0, chunks)),
+                        ((i == 1) & (p == 3), (far, c, c + 1)),
+                        ((i == 1) & (p == 4) & at_end, (last, c, c + 1)),
+                    ]
                 )
-                single = jnp.where((p == n) & at_end, n - 1 - z, -1)
-                u = jnp.where(i == 0, whole, single)
-                low = jnp.where(i == 0, 0, c)
-                high = jnp.where(i == 0, chunks, c + 1)
-
-                @pl.when((u >= 0) & (u < n))
+                slot = jnp.where(i == 0, 0, p - 2)
+
+                @pl.when(u >= 0)
                 def _():
                     def one(cc, carry):
-                        unit_chunk(u, cc)
+                        unit_chunk(slot, u, cc)
                         return carry
 
                     lax.fori_loop(low, high, one, 0)
@@ -513,81 +647,31 @@
             osend[c] = oacc[1, c].astype(jnp.bfloat16)
             x_out(c).start()
 
-        last = jnp.where(at_end, n - 1 - z, -1)
-        back = jnp.where(
-            p == 4,
-            jnp.where(c == 1, z, jnp.where(c == 2, z - 1, jnp.where(c == 3, z + 1, -1))),
-            jnp.where(p == 5, jnp.where(c == 0, far, jnp.where(c == chunks - 2, last, -1)), -1),
-        )
-
-        @pl.when((back >= 0) & (back < n))
-        def _():
-            backward_unit(back)
-
-    each(n * chunks + 1, step)
-
-    def ends(c):
-        def line(d):
-            @pl.when(place(d) < n - 1)
+            @pl.when((c == 1) | (c == 2))
             def _():
-                for p in range(1, n + 1):
-                    along(d, p, c, rs.at[0, 0], rs.at[0, 0]).wait_send()
-
-        each(2, line)
-        x_grad(c).wait_send()
-        x_out(c).wait_send()
-        for level in range(levels):
-            swap(level, c).wait_send()
-
-    each(chunks, ends)
-
-    def unit_ends(u):
-        x_context(u).wait_send()
-        x_back(u).wait_send()
-
-    each(n, unit_ends)
-
-
-def write_kernel(
-    rb, qb, kb, vb, nb, mb, out_hbm, dq_hbm, dk_hbm, dv_hbm, nw_hbm, nm_hbm, hs, cs
-):
-    heads, _, size = qb.shape
-    chunks, _, wide = rb.shape
-
-    def head(h):
-        lanes = pl.ds(pl.multiple_of(h * size, size), size)
-        return [
-            pltpu.make_async_copy(src.at[h], dst.at[:, lanes], hs.at[i, h])
-            for i, (src, dst) in enumerate(((qb, dq_hbm), (kb, dk_hbm), (vb, dv_hbm)))
-        ]
-
-    def chunk(c):
-        lanes = pl.ds(pl.multiple_of(c * wide, wide), wide)
-        return [
-            pltpu.make_async_copy(src.at[c], dst.at[:, lanes], cs.at[i, c])
-            for i, (src, dst) in enumerate(((rb, out_hbm), (nb, nw_hbm), (mb, nm_hbm)))
-        ]
-
-    def start(count, copies):
-        def one(i, carry):
-            for copy in copies(i):
-                copy.start()
-            return carry
-
-        lax.fori_loop(0, count, one, 0)
-
-    def wait(count, copies):
-        def one(i, carry):
-            for copy in copies(i):
-                copy.wait()
-            return carry
-
-        lax.fori_loop(0, count, one, 0)
-
-    start(chunks, chunk)
-    start(heads, head)
-    wait(chunks, chunk)
-    wait(heads, head)
+                backward_heads(jnp.where(c == 1, z, first_side), 0, per)
+
+        @pl.when(p == n + 1)
+        def _():
+            finish(c)
+
+    each(len(order), step)
+    each(n, unit_sent)
+    each_part(chunks - 1, average)
+
+    last_sent(chunks - 1)
+
+
+def write_kernel(*refs):
+    count = len(refs) // 2
+    sems = refs[-1]
+    copies = [
+        pltpu.make_async_copy(refs[i], refs[count + i], sems.at[i]) for i in range(count)
+    ]
+    for copy in copies:
+        copy.start()
+    for copy in copies:
+        copy.wait()
 
 
 def line_shape(count, levels, tokens, features, rows, columns):
@@ -604,6 +688,8 @@
         and 2 * rows * n == features
         and columns % wide == 0
         and columns // wide >= 5
+        and rows % (16 * COARSE) == 0
+        and rows % (16 * FINE) == 0
     )
     return (n, wide) if fits else None
 
@@ -621,18 +707,13 @@
     low, full = jnp.bfloat16, jnp.float32
     dma = pltpu.SemaphoreType.DMA
     like = lambda a: jax.ShapeDtypeStruct(a.shape, a.dtype)
-    by_head = pltpu.VMEM((heads, tokens, HEAD_SIZE), low)
     held = pl.pallas_call(
         functools.partial(line_kernel, n, levels),
-        in_specs=[any_space] * 7 + [in_vmem, pl.BlockSpec(memory_space=pltpu.SMEM)],
+        in_specs=[any_space] * 9,
         out_specs=[in_vmem] * 6,
         out_shape=[
-            pltpu.VMEM((chunks, tokens, wide), low),
-            by_head,
-            by_head,
-            by_head,
-            pltpu.VMEM((chunks, rows, wide), low),
-            pltpu.VMEM((chunks, rows, wide), full),
+            pltpu.VMEM(a.shape, a.dtype)
+            for a in (residual, query, key, value, weight, momentum)
         ],
         scratch_shapes=[
             pltpu.VMEM((n, chunks, rows, wide), low),
@@ -642,7 +723,7 @@
             pltpu.VMEM((n, rows, tokens), low),
             pltpu.VMEM((features, tokens), low),
             pltpu.VMEM((n, rows, tokens), low),
-            pltpu.VMEM((2, rows, tokens), full),
+            pltpu.VMEM((3, 2, rows, tokens), full),
             pltpu.VMEM((2, chunks, tokens, wide), full),
             pltpu.VMEM((chunks, tokens, wide), low),
             pltpu.VMEM((chunks, tokens, wide), low),
@@ -650,6 +731,10 @@
             pltpu.VMEM((chunks, rows, wide), low),
             pltpu.VMEM((levels, chunks, rows, wide), low),
             pltpu.VMEM((tokens, tokens), full),
+            pltpu.VMEM((rows, wide), full),
+            pltpu.VMEM((1, tokens), jnp.int32),
+            pltpu.SMEM((1,), jnp.int32),
+            dma((2,)),
             dma((3, heads)),
             dma((chunks,)),
             dma((chunks,)),
@@ -663,10 +748,12 @@
             dma((n,)),
             dma((chunks,)),
             dma((chunks,)),
-            dma((2, n, chunks)),
-            dma((2, n, chunks)),
-            dma((levels, chunks)),
-            dma((levels, chunks)),
+            dma((2, n - 1, chunks)),
+            dma((2, n - 1, chunks)),
+            dma((2, chunks, FINE)),
+            dma((2, chunks, FINE)),
+            dma((levels, chunks, FINE)),
+            dma((levels, chunks, FINE)),
         ],
         compiler_params=pltpu.CompilerParams(
             collective_id=0, has_side_effects=True, vmem_limit_bytes=50 << 20
@@ -687,7 +774,7 @@
         in_specs=[any_space] * 6,
         out_specs=[any_space] * 6,
         out_shape=[like(a) for a in (residual, query, key, value, weight, momentum)],
-        scratch_shapes=[dma((3, heads)), dma((3, chunks))],
+        scratch_shapes=[dma((6,))],
         compiler_params=pltpu.CompilerParams(vmem_limit_bytes=1 << 20),
     )(*held)
 

time: 165 us -> 162 us (0.982)
  Pallas kernels: 164 us -> 160 us
    pallas_call x1, Pallas kernels: 158 us -> 155 us  [on_line(): pl.pallas_call(functools.partial(line_kernel, n, levels), in_specs=[any_s...]
where the time goes in v3:
time: 162 us
  Pallas kernels  160 us (99%)
    pallas_call x1, Pallas kernels, on_line(): pl.pallas_call(functools.partial(line_kernel, n, levels), in_specs=[any_s...  155 us
    pallas_call x1, Pallas kernels, on_line(): pl.pallas_call(write_kernel, in_specs=[any_space] * 6, out_specs=[any_spa...  4.79 us

profile of v3, /device:TPU:0, one launch (start us, length us, event | category | flops | bytes accessed | tf_op | source)
XLA Modules:
  0.0 161.6 jit_solution(4415633195173002943)
XLA Ops:
  1.3 155.5 %shard_map.136 = (bf16[384,2560]{1,0:T(8,128)(2,1)S(1)}, bf16[384,2560]{1,0:T(8,128)(2,1)S(1)}, bf16[384,2560]{1,0:T(8,128)(2,1)S(1)}, bf16[384,2560]{1,0:T(8,12...) custom-call(bf16[384,2560]{1,0:T(8,128)(2,1)} %bitcast.14, bf16[384,2560]{1,0:T(8,128)(2,1)} %bitcast.15, ...), custom_call_target="tpu_custom_call" | custom-call | tf_op jit(solution)/shard_map/pallas_call | solution.py:710
  156.8 4.8 %shard_map.137 = (bf16[384,2560]{1,0:T(8,128)(2,1)}, bf16[384,2560]{1,0:T(8,128)(2,1)}, bf16[384,2560]{1,0:T(8,128)(2,1)}, bf16[384,2560]{1,0:T(8,128)(2,1)}, bf...) custom-call(bf16[384,2560]{1,0:T(8,128)(2,1)S(1)} %get-tuple-element.18.refs_0_, ...), custom_call_target="tpu_custom_call" | custom-call | tf_op jit(solution)/shard_map/pallas_call | solution.py:772

commit v4 on v3

--- a/solution.py
+++ b/solution.py
@@ -93,7 +93,7 @@
 
 MESH = pl.DeviceIdType.MESH
 LANES = 128
-COARSE, FINE = 2, 2
+PARTS = ((1, 2), (2, 2))
 
 
 def dot(a, b, ca, cb):
@@ -115,7 +115,7 @@
 
 def line_kernel(
     n,
-    levels,
+    level,
     q_hbm,
     k_hbm,
     v_hbm,
@@ -124,7 +124,6 @@
     w_hbm,
     mom_hbm,
     doc_hbm,
-    step_hbm,
     rb,
     qb,
     kb,
@@ -148,7 +147,6 @@
     bias,
     own,
     doc_ref,
-    step_ref,
     ds,
     hs,
     ws,
@@ -174,6 +172,7 @@
     size = HEAD_SIZE
     tokens, heads = qb.shape[0], qb.shape[1] // size
     per = heads // n
+    coarse, fine = PARTS[min(level, 1)]
     scale = HEAD_SIZE ** (-0.5)
     me = lax.axis_index("fsdp")
     rep = lax.axis_index("rep")
@@ -182,9 +181,8 @@
     pair = me + 1 - 2 * x
     at_end = (z == 0) | (z == n - 1)
 
-    def partner(level):
-        bit = lax.rem(lax.div(rep, 1 << level), 2)
-        return rep + (1 << level) - (2 << level) * bit
+    bit = lax.rem(lax.div(rep, 1 << level), 2)
+    partner = rep + (1 << level) - (2 << level) * bit
 
     def lanes(c, width):
         return pl.ds(pl.multiple_of(c * width, width), width)
@@ -198,11 +196,11 @@
     def each_part(c, body):
         @pl.when(c < chunks - 1)
         def _():
-            each(COARSE, lambda s: body(c, s, rows // COARSE))
+            each(coarse, lambda s: body(c, s, rows // coarse))
 
         @pl.when(c == chunks - 1)
         def _():
-            each(FINE, lambda s: body(c, s, rows // FINE))
+            each(fine, lambda s: body(c, s, rows // fine))
 
     def cut_rows(s, part):
         return pl.ds(pl.multiple_of(s * part, 16), part)
@@ -272,13 +270,13 @@
     def place(d):
         return z + d * (n - 1 - 2 * z)
 
-    def swap(level, c, s, part):
+    def swap(c, s, part):
         return pltpu.make_async_remote_copy(
             src_ref=st.at[c, cut_rows(s, part), :],
-            dst_ref=pr.at[level, c, cut_rows(s, part), :],
-            send_sem=ps.at[level, c, s],
-            recv_sem=pr_r.at[level, c, s],
-            device_id={"rep": partner(level)},
+            dst_ref=pr.at[c, cut_rows(s, part), :],
+            send_sem=ps.at[c, s],
+            recv_sem=pr_r.at[c, s],
+            device_id={"rep": partner},
             device_id_type=MESH,
         )
 
@@ -303,10 +301,7 @@
 
     barrier = pltpu.get_barrier_semaphore()
     pl.semaphore_signal(barrier, inc=1, device_id={"fsdp": pair}, device_id_type=MESH)
-    for level in range(levels):
-        pl.semaphore_signal(
-            barrier, inc=1, device_id={"rep": partner(level)}, device_id_type=MESH
-        )
+    pl.semaphore_signal(barrier, inc=1, device_id={"rep": partner}, device_id_type=MESH)
 
     @pl.when(z > 0)
     def _():
@@ -316,7 +311,7 @@
     def _():
         pl.semaphore_signal(barrier, inc=1, device_id={"fsdp": me + 2}, device_id_type=MESH)
 
-    pl.semaphore_wait(barrier, 1 + levels + jnp.where(at_end, 1, 2))
+    pl.semaphore_wait(barrier, 2 + jnp.where(at_end, 1, 2))
 
     def first_sends(c):
         def one(d):
@@ -328,10 +323,8 @@
 
     each(chunks, first_sends)
     x_grad(0).start()
-    load_doc = pltpu.make_async_copy(doc_hbm, doc_ref, ds.at[0])
-    load_step = pltpu.make_async_copy(step_hbm, step_ref, ds.at[1])
+    load_doc = pltpu.make_async_copy(doc_hbm, doc_ref, ds)
     load_doc.start()
-    load_step.start()
     each(n, start_loads)
 
     def other_loads(c):
@@ -343,7 +336,6 @@
     each(chunks, other_loads)
 
     load_doc.wait()
-    load_step.wait()
     row_ids = jnp.broadcast_to(doc_ref[...], (tokens, tokens))
     column_ids = jnp.transpose(row_ids)
     r = lax.broadcasted_iota(jnp.int32, (tokens, tokens), 0)
@@ -466,18 +458,18 @@
         mb[cut, across] = moment
         stepped = wbuf[z, c, cut, :].astype(jnp.float32) - learning_rate * moment
         st[c, cut, :] = stepped.astype(jnp.bfloat16)
-        for level in range(levels):
-            swap(level, c, s, part).start()
-        a, b = min(2, per), min(3, per)
+        swap(c, s, part).start()
+        a, b, e = min(2, per), min(3, per), min(4, per)
+        tip = coarse - 1
         u, low, high = pick(
             [
-                (at_end & (c == 0) & (s == 1), (far, 0, per)),
-                (at_end & (c == chunks - 3) & (s == 1), (last, 0, a)),
-                (at_end & (c == chunks - 2) & (s == 0), (last, a, b)),
-                (at_end & (c == chunks - 2) & (s == 1), (last, b, min(4, per))),
-                (at_end & (c == chunks - 1) & (s == 0), (last, min(4, per), per)),
-                (~at_end & (c == 0) & (s == 1), (z + 1, 0, per)),
-                (~at_end & (c == 1) & (s == 1), (far, 0, per)),
+                (at_end & (c == 0) & (s == tip), (far, 0, per)),
+                (at_end & (c == chunks - 3) & (s == tip), (last, 0, a)),
+                (at_end & (c == chunks - 2) & (s == 0), (last, a, e if coarse == 1 else b)),
+                (at_end & (c == chunks - 2) & (s == 1), (last, b, e)),
+                (at_end & (c == chunks - 1) & (s == fine - 1), (last, e, per)),
+                (~at_end & (c == 0) & (s == tip), (z + 1, 0, per)),
+                (~at_end & (c == 1) & (s == tip), (far, 0, per)),
             ]
         )
 
@@ -487,13 +479,8 @@
 
     def average(c, s, part):
         cut = cut_rows(s, part)
-        for level in range(levels):
-            swap(level, c, s, part).wait()
-        level_now = jnp.full((part, wide), lax.rem(step_ref[0], levels), jnp.int32)
-        other = pr[levels - 1, c, cut, :].astype(jnp.float32)
-        for level in range(levels - 1):
-            before = pr[level, c, cut, :].astype(jnp.float32)
-            other = jnp.where(level_now == level, before, other)
+        swap(c, s, part).wait()
+        other = pr[c, cut, :].astype(jnp.float32)
         mean = (st[c, cut, :].astype(jnp.float32) + other) * 0.5
         nb[cut, lanes(c, wide)] = mean.astype(jnp.bfloat16)
 
@@ -537,19 +524,31 @@
     def finish(c):
         own[...] = weight_part(z, c)
         each_part(c, finish_part)
+
+        @pl.when(c < chunks - 2)
+        def _():
+            finish_out(c)
+
+        @pl.when((c > 0) & (c < chunks - 2))
+        def _():
+            each_part(c - 1, average)
+            last_sent(c - 1)
+
+        @pl.when(c == chunks - 1)
+        def _():
+            finish_out(chunks - 2)
+            finish_out(chunks - 1)
+            for i in (3, 2):
+                each_part(chunks - i, average)
+                last_sent(chunks - i)
+            each(chunks, early_sent)
+            each(n, unit_sent)
+
+    def finish_out(c):
         x_out(c).wait_recv()
         across = lanes(c, wide)
         total_out = rb[:, across].astype(jnp.float32) + oacc[0, c]
         rb[:, across] = (total_out + ogot[c].astype(jnp.float32)).astype(jnp.bfloat16)
-
-        @pl.when(c > 0)
-        def _():
-            each_part(c - 1, average)
-            last_sent(c - 1)
-
-        @pl.when(c == chunks - 2)
-        def _():
-            each(chunks, early_sent)
 
     order = step_order(n, chunks)
 
@@ -656,7 +655,6 @@
             finish(c)
 
     each(len(order), step)
-    each(n, unit_sent)
     each_part(chunks - 1, average)
 
     last_sent(chunks - 1)
@@ -688,28 +686,27 @@
         and 2 * rows * n == features
         and columns % wide == 0
         and columns // wide >= 5
-        and rows % (16 * COARSE) == 0
-        and rows % (16 * FINE) == 0
+        and all(rows % (16 * part) == 0 for parts in PARTS for part in parts)
     )
     return (n, wide) if fits else None
 
 
 def on_line(
-    n, wide, query, key, value, residual, out_grad, doc_ids, weight, momentum, step_index
+    n, wide, level, query, key, value, residual, out_grad, doc_ids, weight, momentum
 ):
     tokens, features = query.shape
     rows, columns = weight.shape
     chunks = columns // wide
     heads = features // HEAD_SIZE
-    levels = lax.axis_size("rep").bit_length() - 1
     any_space = pl.BlockSpec(memory_space=pl.ANY)
     in_vmem = pl.BlockSpec(memory_space=pltpu.VMEM)
+    fine = max(PARTS[min(level, 1)])
     low, full = jnp.bfloat16, jnp.float32
     dma = pltpu.SemaphoreType.DMA
     like = lambda a: jax.ShapeDtypeStruct(a.shape, a.dtype)
     held = pl.pallas_call(
-        functools.partial(line_kernel, n, levels),
-        in_specs=[any_space] * 9,
+        functools.partial(line_kernel, n, level),
+        in_specs=[any_space] * 8,
         out_specs=[in_vmem] * 6,
         out_shape=[
             pltpu.VMEM(a.shape, a.dtype)
@@ -729,12 +726,11 @@
             pltpu.VMEM((chunks, tokens, wide), low),
             pltpu.VMEM((n + 1, chunks, rows, wide), low),
             pltpu.VMEM((chunks, rows, wide), low),
-            pltpu.VMEM((levels, chunks, rows, wide), low),
+            pltpu.VMEM((chunks, rows, wide), low),
             pltpu.VMEM((tokens, tokens), full),
             pltpu.VMEM((rows, wide), full),
             pltpu.VMEM((1, tokens), jnp.int32),
-            pltpu.SMEM((1,), jnp.int32),
-            dma((2,)),
+            dma(()),
             dma((3, heads)),
             dma((chunks,)),
             dma((chunks,)),
@@ -750,13 +746,13 @@
             dma((chunks,)),
             dma((2, n - 1, chunks)),
             dma((2, n - 1, chunks)),
-            dma((2, chunks, FINE)),
-            dma((2, chunks, FINE)),
-            dma((levels, chunks, FINE)),
-            dma((levels, chunks, FINE)),
+            dma((2, chunks, fine)),
+            dma((2, chunks, fine)),
+            dma((chunks, fine)),
+            dma((chunks, fine)),
         ],
         compiler_params=pltpu.CompilerParams(
-            collective_id=0, has_side_effects=True, vmem_limit_bytes=50 << 20
+            collective_id=level, has_side_effects=True, vmem_limit_bytes=50 << 20
         ),
     )(
         query,
@@ -767,7 +763,6 @@
         weight,
         momentum,
         doc_ids,
-        step_index,
     )
     return pl.pallas_call(
         write_kernel,
@@ -801,8 +796,14 @@
     )
     if shape is not None:
         arrays = (query_rows, key_rows, value_rows, residual_in, out_grad)
-        results = on_line(
-            *shape, *[a[0] for a in arrays], doc_ids, out_weight[0], momentum[0], step_index
+        levels = lax.axis_size("rep").bit_length() - 1
+        results = lax.switch(
+            lax.rem(step_index[0].astype(jnp.uint32), jnp.uint32(levels)).astype(jnp.int32),
+            [functools.partial(on_line, *shape, level) for level in range(levels)],
+            *[a[0] for a in arrays],
+            doc_ids,
+            out_weight[0],
+            momentum[0],
         )
         return tuple(r[None] for r in results)
     side = lax.axis_index("fsdp") % 2

time: 162 us -> 159 us (0.981); the launches traced: 162 us -> 157 us
  Pallas kernels: 160 us -> 155 us
    pallas_call x1, Pallas kernels: 155 us -> 150 us  [on_line(): pl.pallas_call(functools.partial(line_kernel, n, level), in_specs=[any_sp...]
where the time goes in v4:
time: 159 us; the launch traced here: 157 us
  Pallas kernels  155 us (97%)
    pallas_call x1, Pallas kernels, on_line(): pl.pallas_call(functools.partial(line_kernel, n, level), in_specs=[any_sp...  150 us
    pallas_call x1, Pallas kernels, on_line(): pl.pallas_call(write_kernel, in_specs=[any_space] * 6, out_specs=[any_spa...  4.79 us

profile of v4, /device:TPU:0, one launch (start us, length us, event | category | flops | bytes accessed | tf_op | source)
XLA Modules:
  0.0 156.7 jit_solution(7402081260702059432)
XLA Ops:
  1.3 155.3 %conditional.1 = ((bf16[384,2560]{1,0:T(8,128)(2,1)}, bf16[384,2560]{1,0:T(8,128)(2,1)}, bf16[384,2560]{1,0:T(8,128)(2,1)}, bf16[384,2560]{1,0:T(8,128)(2,1)}, b...) conditional(s32[]{:T(128)} %bitcast, (bf16[384,2560]{1,0:T(8,128)(2,1)}, bf16[384,2560]{1,0:T(8,128)(2,1)}, ...), branch_computations={%region_0.0_spmd.clone, %region_1.0_spmd.clone} | conditional | bytes 8 | solution.py:800
  1.3 150.2 %branch_0_fun.2 = (bf16[384,2560]{1,0:T(8,128)(2,1)S(1)}, bf16[384,2560]{1,0:T(8,128)(2,1)S(1)}, bf16[384,2560]{1,0:T(8,128)(2,1)S(1)}, bf16[384,2560]{1,0:T(8,1...) custom-call(bf16[384,2560]{1,0:T(8,128)(2,1)} %get-tuple-element.104.q_hbm, ...), custom_call_target="tpu_custom_call" | custom-call | tf_op jit(solution)/shard_map/cond/branch_0_fun/pallas_call | solution.py:707
  151.5 4.8 %branch_0_fun.3 = (bf16[384,2560]{1,0:T(8,128)(2,1)}, bf16[384,2560]{1,0:T(8,128)(2,1)}, bf16[384,2560]{1,0:T(8,128)(2,1)}, bf16[384,2560]{1,0:T(8,128)(2,1)}, b...) custom-call(bf16[384,2560]{1,0:T(8,128)(2,1)S(1)} %get-tuple-element.112.refs_0_, ...), custom_call_target="tpu_custom_call" | custom-call | tf_op jit(solution)/shard_map/cond/branch_0_fun/pallas_call | solution.py:767
